TPU v7x, 512 devices: a whole 4x8x8 slice. The times are simulated.
512 devices in a mesh: dp: 64 (over z, y), own: 8 (over x, core).
Axes of the slice: x: 4, y: 8, z: 8, core: 2. Of those that a mesh axis runs over, the one named last changes fastest.
Arguments:
- partial_grads: bfloat16 [64, 112, 16, 4096], P('dp', None, 'own'), may hold values from -1 to 1
- owner_group: int32 [112], replicated, may hold values from 0 to 63, as said below
- master: float32 [128, 16, 4096], P('dp', 'own'), may hold values from -12 to 12
- moment_one: float32 [128, 16, 4096], P('dp', 'own'), may hold values from -3 to 3
- moment_two: float32 [128, 16, 4096], P('dp', 'own'), may hold values from 0.01 to 1
- vec_grads: bfloat16 [64, 64, 4096], P('dp', None, 'own'), may hold values from -1 to 1
- vec_master: float32 [64, 4096], P(None, 'own'), may hold values from 0.5 to 1.5
- vec_first: float32 [64, 4096], P(None, 'own'), may hold values from -3 to 3
- vec_second: float32 [64, 4096], P(None, 'own'), may hold values from 0.01 to 1
Outputs:
- new_master: float32 [128, 16, 4096], P('dp', 'own')
- new_first: float32 [128, 16, 4096], P('dp', 'own')
- new_second: float32 [128, 16, 4096], P('dp', 'own')
- weights: bfloat16 [112, 16, 4096], P(None, 'own')
- new_vec_master: float32 [64, 4096], P(None, 'own')
- new_vec_first: float32 [64, 4096], P(None, 'own')
- new_vec_second: float32 [64, 4096], P(None, 'own')
Inputs may be any that keep to these rules, and one draw needn't show every extreme that they name: `owner_group`: each owner group is named by at most 2 matrices, and some group by exactly 2.
All inputs are finite; a program needn't handle non-finite values.
Results may differ from a plain program's by a relative error of at most 0.001.
Values may be sent and summed in bfloat16 or wider, within the bound.
No kernel may reach another device: no remote copies, remote signals or barrier semaphores. Data moves between devices by JAX's collectives and lax.ppermute only.
A program may use at most 64 MiB of HBM per device.

v0:
```python
import jax
import jax.numpy as jnp
from jax import lax
from jax.sharding import PartitionSpec as P

beta_one = 0.9
beta_two = 0.95
fix_one = 1.0 - 0.9**10
fix_two = 1.0 - 0.95**10
epsilon = 1e-06
decay_rate = 0.1
learn_rate = 0.05


def slot_numbers(owner_group, capacity):
    count = owner_group.shape[0]
    places = jnp.arange(count, dtype=jnp.int32)
    same = owner_group[:, None] == owner_group[None, :]
    before = places[None, :] < places[:, None]
    ranks = jnp.sum((same & before).astype(jnp.int32), axis=1)
    return owner_group * capacity + ranks


def body(
    partial_grads,
    owner_group,
    master,
    moment_one,
    moment_two,
    vec_grads,
    vec_master,
    vec_first,
    vec_second,
):
    groups = lax.axis_size("dp")
    capacity = master.shape[0]
    slot_count = groups * capacity
    slots = slot_numbers(owner_group, capacity)
    matches = slots[None, :] == jnp.arange(slot_count, dtype=jnp.int32)[:, None]
    source = jnp.sum(
        matches.astype(jnp.int32) * jnp.arange(owner_group.shape[0], dtype=jnp.int32)[None, :],
        axis=1,
    )
    occupied = jnp.any(matches, axis=1)
    weight_sq = jnp.sum(master * master, axis=(1, 2))
    sectioned = jnp.take(partial_grads[0], source, axis=0)
    sectioned = jnp.where(occupied[:, None, None], sectioned, jnp.zeros_like(sectioned))
    gradient = lax.psum_scatter(
        sectioned.astype(jnp.float32), "dp", scatter_dimension=0, tiled=True
    )
    my_group = lax.axis_index("dp")
    mine = lax.dynamic_slice_in_dim(occupied, my_group * capacity, capacity)[:, None, None]
    first_raw = beta_one * moment_one + (1.0 - beta_one) * gradient
    second_raw = beta_two * moment_two + (1.0 - beta_two) * gradient * gradient
    update = first_raw / fix_one / (jnp.sqrt(second_raw / fix_two) + epsilon) + decay_rate * master
    update_sq = jnp.sum(update * update, axis=(1, 2))
    weight_total, update_total = lax.psum((weight_sq, update_sq), "own")
    ratio = jnp.sqrt(weight_total) / jnp.sqrt(update_total)
    stepped = master - learn_rate * ratio[:, None, None] * update
    zeros_block = jnp.zeros_like(master)
    new_master = jnp.where(mine, stepped, zeros_block)
    new_first = jnp.where(mine, first_raw, zeros_block)
    new_second = jnp.where(mine, second_raw, zeros_block)
    published = lax.all_gather(new_master.astype(jnp.bfloat16), "dp", axis=0, tiled=True)
    weights = jnp.take(published, slots, axis=0)
    vec_gradient = lax.psum(vec_grads[0].astype(jnp.float32), "dp")
    new_vec_first = beta_one * vec_first + (1.0 - beta_one) * vec_gradient
    new_vec_second = beta_two * vec_second + (1.0 - beta_two) * vec_gradient * vec_gradient
    new_vec_master = vec_master - learn_rate * (new_vec_first / fix_one) / (
        jnp.sqrt(new_vec_second / fix_two) + epsilon
    )
    return (
        new_master,
        new_first,
        new_second,
        weights,
        new_vec_master,
        new_vec_first,
        new_vec_second,
    )


def solution(mesh):
    placed = (
        P("dp", None, "own", None),
        P(),
        P("dp", "own", None),
        P("dp", "own", None),
        P("dp", "own", None),
        P("dp", None, "own"),
        P(None, "own"),
        P(None, "own"),
        P(None, "own"),
    )
    return jax.shard_map(
        body,
        mesh=mesh,
        in_specs=placed,
        out_specs=(
            P("dp", "own", None),
            P("dp", "own", None),
            P("dp", "own", None),
            P(None, "own", None),
            P(None, "own"),
            P(None, "own"),
            P(None, "own"),
        ),
        check_vma=False,
    )
```

profile of v0, /device:TPU:4, one launch (start us, length us, event | category | flops | bytes accessed | tf_op | source)
XLA Modules:
  0.0 314.6 jit_solution(13815475503733527499)
XLA Ops:
  7.2 0.0 copy-start
  7.2 0.0 all-reduce.5.cloned.1.call-start
  7.2 1.0 convert_reduce_fusion
  8.2 0.7 compare_and_fusion
  8.9 0.1 select_reduce_fusion
  9.0 0.1 fusion.3
  9.1 1.5 bitcast_convert_fusion
  10.6 0.0 copy-done
  10.6 8.0 %gather_fusion = bf16[128,2,4096]{2,1,0:T(2,128)(2,1)} fusion(bf16[112,2,4096]{2,1,0:T(2,128)(2,1)S(1)} %bitcast.9, s32[1024]{0:T(1024)S(1)} %pad_clamp_fusion.1), kind=kCustom, calls=%fused_computation | custom fusion | bytes 4194816 | tf_op jit(solution)/shard_map/jit(_take)/gather | solution.py:46
  18.6 5.7 %fusion = f32[128,2,4096]{2,1,0:T(2,128)} fusion(pred[128]{0:T(512)(128)(4,1)S(1)} %fusion.3, bf16[128,2,4096]{2,1,0:T(2,128)(2,1)} %gather_fusion, pred[128]{0:T(512)(128)(4,1)S(1)} %compare_and_fusion.1), kind=kLoop, calls=%fused_computation.5 | loop fusion | flops 3145728 | bytes 6291712 | tf_op jit(solution)/shard_map/convert_element_type | solution.py:49
  24.4 0.0 copy-start.1
  24.4 0.0 copy-start.5
  24.4 0.0 copy-start.6
  24.4 0.0 copy-start.2
  24.4 0.0 copy-start.3
  24.4 0.0 copy-start.4
  24.4 0.0 all-reduce.5.cloned.1.call-update
  24.4 0.0 all-gather.2.cloned.1.call-start
  24.5 0.1 dynamic_slice.3
  24.6 1.3 dynamic-slice
  26.6 173.7 %all-reduce.5.cloned.1.call-done = (f32[128,2,4096]{2,1,0:T(2,128)}, f32[64,512]{1,0:T(8,128)}) async-done(((f32[128,2,4096]{2,1,0:T(2,128)}, f32[64,512]{1,0:T(8,128)}), (f32[128,2,4096]{2,1,0:T(2,128)}, f32[64,512]{1,0:T(8,128)})) %all-reduce.5.cloned.1.call-update) | async-done | bytes 4325392
  200.2 0.0 copy-done.1
  200.2 0.0 copy-done.5
  200.2 0.0 copy-done.6
  200.2 1.9 multiply_reduce_fusion
  202.1 10.2 %all-reduce.2 = (f32[2]{0:T(128)S(1)}, f32[2]{0:T(128)S(1)}) all-reduce(f32[2]{0:T(128)S(1)} %get-tuple-element.18, f32[2]{0:T(128)S(1)} %get-tuple-element.22), channel_id=1, replica_groups=mesh['dp'=64,'own'=8] {'own'}, use_global_device_ids=true, to_apply=%region_7.8 | all-reduce | flops 4 | bytes 32 | tf_op jit(solution)/shard_map/psum | solution.py:57
  212.4 0.8 fusion.7
  213.1 0.0 all-gather.2.cloned.1.call-update
  213.2 0.0 copy-done.2
  213.2 0.0 copy-done.3
  213.2 0.0 copy-done.4
  213.2 1.7 divide_subtract_fusion
  214.9 78.8 %all-gather.2.cloned.1.call-done = bf16[128,2,4096]{2,1,0:T(2,128)(2,1)} async-done(((bf16[2,2,4096]{2,1,0:T(2,128)(2,1)}), bf16[128,2,4096]{2,1,0:T(2,128)(2,1)}) %all-gather.2.cloned.1.call-update) | async-done | bytes 2097168 | tf_op jit(solution)/shard_map/all_gather | solution.py:64
  293.7 9.5 %gather_fusion.1 = bf16[112,2,4096]{2,1,0:T(2,128)(2,1)} fusion(bf16[128,2,4096]{2,1,0:T(2,128)(2,1)} %all-gather.2.cloned.1.call-done, s32[1024]{0:T(1024)S(1)} %pad_clamp_fusion), kind=kCustom, calls=%fused_computation.1 | custom fusion | bytes 3670464 | tf_op jit(solution)/shard_map/jit(_take)/gather | solution.py:65
  303.2 4.5 %broadcast_select_fusion.2 = bf16[112,2,4096]{2,1,0:T(2,128)(2,1)} fusion(bf16[112,2,4096]{2,1,0:T(2,128)(2,1)} %gather_fusion.1, pred[112]{0:T(512)(128)(4,1)S(1)} %get-tuple-element.14), kind=kLoop, calls=%fused_computation.4 | loop fusion | flops 917504 | bytes 3670128 | tf_op jit(solution)/shard_map/jit(_take)/select_n | solution.py:65
  (6 shorter events, 0.0 us)
Async XLA Ops:
  7.2 3.5 %copy-start = (bf16[1,112,2,4096]{3,2,1,0:T(2,128)(2,1)S(1)}, bf16[1,112,2,4096]{3,2,1,0:T(2,128)(2,1)}, u32[]{:S(2)}) copy-start(bf16[1,112,2,4096]{3,2,1,0:T(2,128)(2,1)} %param.9) | copy-start | bytes 5505028
  7.2 193.1 %all-reduce.5.cloned.1.call-start = ((), (), s32[]{:S(2)}) async-start(), calls=%async_computation.1 | async-start | bytes 8650752
  24.4 175.9 %copy-start.1 = (f32[2,2,4096]{2,1,0:T(2,128)S(1)}, f32[2,2,4096]{2,1,0:T(2,128)}, u32[]{:S(2)}) copy-start(f32[2,2,4096]{2,1,0:T(2,128)} %param.11) | copy-start | bytes 196612
  24.4 175.9 %copy-start.5 = (f32[2,2,4096]{2,1,0:T(2,128)S(1)}, f32[2,2,4096]{2,1,0:T(2,128)}, u32[]{:S(2)}) copy-start(f32[2,2,4096]{2,1,0:T(2,128)} %param.13) | copy-start | bytes 196612
  24.4 175.9 %copy-start.6 = (f32[2,2,4096]{2,1,0:T(2,128)S(1)}, f32[2,2,4096]{2,1,0:T(2,128)}, u32[]{:S(2)}) copy-start(f32[2,2,4096]{2,1,0:T(2,128)} %param.12) | copy-start | bytes 196612
  24.4 188.8 %copy-start.2 = (f32[64,512]{1,0:T(8,128)S(1)}, f32[64,512]{1,0:T(8,128)}, u32[]{:S(2)}) copy-start(f32[64,512]{1,0:T(8,128)} %param.15) | copy-start | bytes 393220
  24.4 188.8 %copy-start.3 = (f32[64,512]{1,0:T(8,128)S(1)}, f32[64,512]{1,0:T(8,128)}, u32[]{:S(2)}) copy-start(f32[64,512]{1,0:T(8,128)} %param.16) | copy-start | bytes 393220
  24.4 188.8 %copy-start.4 = (f32[64,512]{1,0:T(8,128)S(1)}, f32[64,512]{1,0:T(8,128)}, u32[]{:S(2)}) copy-start(f32[64,512]{1,0:T(8,128)} %param.17) | copy-start | bytes 393220
  24.4 269.3 %all-gather.2.cloned.1.call-start = ((), (), s32[]{:S(2)}) async-start(), calls=%async_computation | async-start | bytes 2129920 | tf_op jit(solution)/shard_map/all_gather | solution.py:64
Sparse Core Ops, SparseCore 0:
  24.6 175.6 all-reduce.4
  213.3 80.4 all-gather.1
where the time goes:
time: 315 us
  waiting for transfers between devices  253 us (80%)
  local copies, waits for them, and re-layouts  19 us (6%)
  other arithmetic  18 us (6%)
  between operations  14.8 us (5%)
  blocking collectives  10.2 us (3%)
    unnamed x3, waiting for transfers between devices  174 us
    all_gather x1, waiting for transfers between devices, body(): lax.all_gather(new_master.astype(jnp.bfloat16), 'dp', axis=0, tiled=True)  78.8 us
    psum x1, blocking collectives, body(): weight_total, update_total = lax.psum((weight_sq, update_sq), 'own')  10.2 us
    gather x1, local copies, waits for them, and re-layouts, body(): weights = jnp.take(published, slots, axis=0)  9.48 us
    gather x1, local copies, waits for them, and re-layouts, body(): sectioned = jnp.take(partial_grads[0], source, axis=0)  8.02 us
  transfers between devices with their start and end apart: 2, of which 2 were waited for; matrix products, arithmetic and copies ran while one was open for 1% of the time, Pallas kernels for 0%

commit v1 on v0

v1 whole, which is shorter than its diff:
```python
import functools

import jax
import jax.numpy as jnp
from jax import lax
from jax.experimental import pallas as pl
from jax.experimental.pallas import tpu as pltpu
from jax.sharding import PartitionSpec as P

beta_one = 0.9
beta_two = 0.95
fix_one = 1.0 - 0.9**10
fix_two = 1.0 - 0.95**10
epsilon = 1e-06
decay_rate = 0.1
learn_rate = 0.05

SIDE = 8
CAP = 2
LANES = 128
ROWS = 64
SLOT_ROWS = CAP * ROWS
VEC_ROWS = 4
PART = SIDE * SLOT_ROWS
WIDE = PART + SIDE * VEC_ROWS
CHUNK = SLOT_ROWS + 2 * VEC_ROWS

VMEM = pl.BlockSpec(memory_space=pltpu.VMEM)
SMEM = pl.BlockSpec(memory_space=pltpu.SMEM)
ANY = pl.BlockSpec(memory_space=pl.ANY)


def place_of(group):
    core = lax.rem(lax.axis_index("own"), 2)
    z, y = group // SIDE, lax.rem(group, SIDE)
    return jnp.where(core == 0, y, z), jnp.where(core == 0, z, y)


def pack_kernel(owner, grads, vecs, out, held, sem, vec_sem):
    count = owner.shape[0]

    def clear(g, _):
        held[g] = 0
        return 0

    lax.fori_loop(0, SIDE * SIDE, clear, 0, unroll=8)
    vec_copy = pltpu.make_async_copy(vecs, out.at[:, pl.ds(PART, SIDE * VEC_ROWS), :], vec_sem)
    vec_copy.start()

    def send(m, _):
        g = owner[m]
        rank = held[g]
        held[g] = rank + 1
        far, near = place_of(g)
        row = pl.multiple_of(near * SLOT_ROWS + rank * ROWS, ROWS)
        pltpu.make_async_copy(grads.at[m], out.at[far, pl.ds(row, ROWS), :], sem).start()
        return 0

    lax.fori_loop(0, count, send, 0, unroll=4)

    def empty(g, _):
        far, near = place_of(g)
        for rank in range(CAP):

            @pl.when(held[g] <= rank)
            def _():
                row = pl.multiple_of(near * SLOT_ROWS + rank * ROWS, ROWS)
                out[far, pl.ds(row, ROWS), :] = jnp.zeros((ROWS, LANES), out.dtype)

        return 0

    lax.fori_loop(0, SIDE * SIDE, empty, 0, unroll=2)
    vec_copy.wait()
    pltpu.make_async_copy(grads, grads, sem).wait()


def partial_sum_kernel(got, out):
    for near in range(SIDE):
        rows = pl.ds(near * SLOT_ROWS, SLOT_ROWS)
        total = got[0, rows, :].astype(jnp.float32)
        for far in range(1, SIDE):
            total = total + got[far, rows, :].astype(jnp.float32)
        out[near, pl.ds(0, SLOT_ROWS), :] = total
    total = got[0, pl.ds(PART, SIDE * VEC_ROWS), :].astype(jnp.float32)
    for far in range(1, SIDE):
        total = total + got[far, pl.ds(PART, SIDE * VEC_ROWS), :].astype(jnp.float32)
    for near in range(SIDE):
        out[near, pl.ds(SLOT_ROWS, VEC_ROWS), :] = total[near * VEC_ROWS : (near + 1) * VEC_ROWS]
        out[near, pl.ds(SLOT_ROWS + VEC_ROWS, VEC_ROWS), :] = jnp.zeros((VEC_ROWS, LANES), jnp.float32)


def update_kernel(held, got, master, one, two, new_first, new_second, update_out, norms, vec_out):
    mine = held[lax.axis_index("dp")]
    for slot in range(CAP):
        rows = pl.ds(slot * ROWS, ROWS)
        gradient = got[0, rows, :]
        for k in range(1, SIDE):
            gradient = gradient + got[k, rows, :]
        weight = master[rows, :]
        first = beta_one * one[rows, :] + (1.0 - beta_one) * gradient
        second = beta_two * two[rows, :] + (1.0 - beta_two) * gradient * gradient
        update = first / fix_one / (jnp.sqrt(second / fix_two) + epsilon) + decay_rate * weight
        keep = mine > slot
        new_first[rows, :] = jnp.where(keep, first, 0.0)
        new_second[rows, :] = jnp.where(keep, second, 0.0)
        update_out[rows, :] = update
        weight_sq = jnp.sum((weight * weight).reshape(ROWS // 8, 8, LANES), axis=0)
        update_sq = jnp.sum((update * update).reshape(ROWS // 8, 8, LANES), axis=0)
        for k in range(SIDE):
            norms[k, pl.ds(2 * slot, 1), :] = jnp.sum(weight_sq, axis=0, keepdims=True)
            norms[k, pl.ds(2 * slot + 1, 1), :] = jnp.sum(update_sq, axis=0, keepdims=True)
    for k in range(SIDE):
        norms[k, pl.ds(2 * CAP, 8 - 2 * CAP), :] = jnp.zeros((8 - 2 * CAP, LANES), jnp.float32)
    rows = pl.ds(SLOT_ROWS, VEC_ROWS)
    total = got[0, rows, :]
    for k in range(1, SIDE):
        total = total + got[k, rows, :]
    vec_out[pl.ds(0, VEC_ROWS), :] = total
    vec_out[pl.ds(VEC_ROWS, VEC_ROWS), :] = total - total.astype(jnp.bfloat16).astype(jnp.float32)


def step_kernel(held, norms, master, update, vec, new_master, out):
    mine = held[lax.axis_index("dp")]
    total = norms[0]
    for k in range(1, SIDE):
        total = total + norms[k]
    total = jnp.sum(total, axis=1, keepdims=True)
    for slot in range(CAP):
        rows = pl.ds(slot * ROWS, ROWS)
        ratio = jnp.sqrt(total[2 * slot : 2 * slot + 1]) / jnp.sqrt(total[2 * slot + 1 : 2 * slot + 2])
        stepped = master[rows, :] - learn_rate * ratio * update[rows, :]
        stepped = jnp.where(mine > slot, stepped, 0.0)
        new_master[rows, :] = stepped
        rounded = stepped.astype(jnp.bfloat16)
        for k in range(SIDE):
            out[k, rows, :] = rounded
    rounded = vec[...].astype(jnp.bfloat16)
    for k in range(SIDE):
        out[k, pl.ds(SLOT_ROWS, 2 * VEC_ROWS), :] = rounded


def repeat_kernel(got, out):
    for near in range(SIDE):
        block = got[near]
        for k in range(SIDE):
            out[k, pl.ds(near * CHUNK, CHUNK), :] = block


def unpack_kernel(owner, got, vec_master, vec_first, vec_second, weights, new_master, new_first, new_second, held, sem):
    count = owner.shape[0]

    def clear(g, _):
        held[g] = 0
        return 0

    lax.fori_loop(0, SIDE * SIDE, clear, 0, unroll=8)

    def fetch(m, _):
        g = owner[m]
        rank = held[g]
        held[g] = rank + 1
        far, near = place_of(g)
        row = pl.multiple_of(near * CHUNK + rank * ROWS, 8)
        pltpu.make_async_copy(got.at[far, pl.ds(row, ROWS), :], weights.at[m], sem).start()
        return 0

    lax.fori_loop(0, count, fetch, 0, unroll=4)
    for far in range(SIDE):
        pieces = []
        for near in range(SIDE):
            both = got[far, pl.ds(near * CHUNK + SLOT_ROWS, 2 * VEC_ROWS), :].astype(jnp.float32)
            pieces.append(both[:VEC_ROWS] + both[VEC_ROWS:])
        gradient = jnp.concatenate(pieces, axis=0)
        first = beta_one * vec_first[far] + (1.0 - beta_one) * gradient
        second = beta_two * vec_second[far] + (1.0 - beta_two) * gradient * gradient
        new_first[far] = first
        new_second[far] = second
        new_master[far] = vec_master[far] - learn_rate * (first / fix_one) / (jnp.sqrt(second / fix_two) + epsilon)
    pltpu.make_async_copy(weights, weights, sem).wait()


def to_rows(block):
    n, r, columns = block.shape
    return block.reshape(n, r, columns // LANES, LANES).transpose(0, 2, 1, 3).reshape(n, ROWS, LANES)


def from_rows(rows):
    n = rows.shape[0]
    return rows.reshape(n, ROWS // 2, 2, LANES).transpose(0, 2, 1, 3).reshape(n, 2, ROWS // 2 * LANES)


def vec_rows(block):
    return block.reshape(SIDE, SIDE, 4, LANES).transpose(0, 2, 1, 3).reshape(SIDE, 4 * SIDE, LANES)


def from_vec_rows(rows):
    return rows.reshape(SIDE, 4, SIDE, LANES).transpose(0, 2, 1, 3).reshape(SIDE * SIDE, 4 * LANES)


def axis_groups():
    def device(z, y, x, core):
        return (z * SIDE + y) * 8 + x * 2 + core

    side = range(SIDE)

    def along_y(core):
        return [[device(z, y, x, core) for y in side] for z in side for x in range(4)]

    def along_z(core):
        return [[device(z, y, x, core) for z in side] for y in side for x in range(4)]

    return along_y(0) + along_z(1), along_z(0) + along_y(1)


def exchange(x, groups):
    return lax.all_to_all(x, ("dp", "own"), 0, 0, axis_index_groups=groups, tiled=True)


def vmem(shape, dtype):
    return pltpu.VMEM(shape, dtype)


def body(
    partial_grads,
    owner_group,
    master,
    moment_one,
    moment_two,
    vec_grads,
    vec_master,
    vec_first,
    vec_second,
):
    f32, bf16 = jnp.float32, jnp.bfloat16
    first_groups, second_groups = axis_groups()
    count = owner_group.shape[0]
    packed, held = pl.pallas_call(
        pack_kernel,
        out_shape=(jax.ShapeDtypeStruct((SIDE, WIDE, LANES), bf16), jax.ShapeDtypeStruct((SIDE * SIDE,), jnp.int32)),
        in_specs=[SMEM, ANY, ANY],
        out_specs=(VMEM, SMEM),
        scratch_shapes=[pltpu.SemaphoreType.DMA, pltpu.SemaphoreType.DMA],
        name="pack",
    )(owner_group, to_rows(partial_grads[0]), vec_rows(vec_grads[0]))
    got = exchange(packed, first_groups)
    partial = pl.pallas_call(
        partial_sum_kernel,
        out_shape=jax.ShapeDtypeStruct((SIDE, CHUNK, LANES), f32),
        in_specs=[VMEM],
        out_specs=VMEM,
        name="partial_sum",
    )(got)
    got = exchange(partial, second_groups)
    block = jax.ShapeDtypeStruct((SLOT_ROWS, LANES), f32)
    master_rows = to_rows(master).reshape(SLOT_ROWS, LANES)
    new_first, new_second, update, norms, vec_sum = pl.pallas_call(
        update_kernel,
        out_shape=(
            block,
            block,
            block,
            jax.ShapeDtypeStruct((SIDE, 8, LANES), f32),
            jax.ShapeDtypeStruct((2 * VEC_ROWS, LANES), f32),
        ),
        in_specs=[SMEM] + [VMEM] * 4,
        out_specs=(VMEM,) * 5,
        name="update",
    )(
        held,
        got,
        master_rows,
        to_rows(moment_one).reshape(SLOT_ROWS, LANES),
        to_rows(moment_two).reshape(SLOT_ROWS, LANES),
    )
    norms = lax.all_to_all(norms, "own", 0, 0, tiled=True)
    new_master, out = pl.pallas_call(
        step_kernel,
        out_shape=(block, jax.ShapeDtypeStruct((SIDE, CHUNK, LANES), bf16)),
        in_specs=[SMEM] + [VMEM] * 4,
        out_specs=(VMEM, VMEM),
        name="step",
    )(held, norms, master_rows, update, vec_sum)
    got = exchange(out, second_groups)
    out = pl.pallas_call(
        repeat_kernel,
        out_shape=jax.ShapeDtypeStruct((SIDE, SIDE * CHUNK, LANES), bf16),
        in_specs=[VMEM],
        out_specs=VMEM,
        name="repeat",
    )(got)
    got = exchange(out, first_groups)
    vec_block = jax.ShapeDtypeStruct((SIDE, 4 * SIDE, LANES), f32)
    weights, new_vec_master, new_vec_first, new_vec_second = pl.pallas_call(
        unpack_kernel,
        out_shape=(jax.ShapeDtypeStruct((count, ROWS, LANES), bf16), vec_block, vec_block, vec_block),
        in_specs=[SMEM, VMEM, VMEM, VMEM, VMEM],
        out_specs=(ANY, VMEM, VMEM, VMEM),
        scratch_shapes=[pltpu.SMEM((SIDE * SIDE,), jnp.int32), pltpu.SemaphoreType.DMA],
        name="unpack",
    )(owner_group, got, vec_rows(vec_master), vec_rows(vec_first), vec_rows(vec_second))

    def slots(rows):
        return from_rows(rows.reshape(CAP, ROWS, LANES))

    return (
        slots(new_master),
        slots(new_first),
        slots(new_second),
        from_rows(weights),
        from_vec_rows(new_vec_master),
        from_vec_rows(new_vec_first),
        from_vec_rows(new_vec_second),
    )


def solution(mesh):
    placed = (
        P("dp", None, "own", None),
        P(),
        P("dp", "own", None),
        P("dp", "own", None),
        P("dp", "own", None),
        P("dp", None, "own"),
        P(None, "own"),
        P(None, "own"),
        P(None, "own"),
    )
    return jax.shard_map(
        body,
        mesh=mesh,
        in_specs=placed,
        out_specs=(
            P("dp", "own", None),
            P("dp", "own", None),
            P("dp", "own", None),
            P(None, "own", None),
            P(None, "own"),
            P(None, "own"),
            P(None, "own"),
        ),
        check_vma=False,
    )
```

time: 315 us -> 141 us (0.45)
  the two profiles are of different devices: /device:TPU:4 before, /device:TPU:2 now
where the time goes in v1:
time: 141 us
  blocking collectives  122 us (87%)
  Pallas kernels  18.4 us (13%)
    all_to_all x4, blocking collectives, exchange(): lax.all_to_all(x, ('dp', 'own'), 0, 0, axis_index_groups=groups, tiled=True)  113 us
    all_to_all x1, blocking collectives, body(): norms = lax.all_to_all(norms, 'own', 0, 0, tiled=True)  8.92 us
    pallas_call x1, Pallas kernels, body(): pl.pallas_call(pack_kernel, out_shape=(jax.ShapeDtypeStruct((SIDE, WIDE,...  4.95 us
    pallas_call x1, Pallas kernels, body(): pl.pallas_call(unpack_kernel, out_shape=(jax.ShapeDtypeStruct((count, ROW...  4.48 us

profile of v1, /device:TPU:2, one launch (start us, length us, event | category | flops | bytes accessed | tf_op | source)
XLA Modules:
  0.0 140.6 jit_solution(896572610169615695)
XLA Ops:
  0.6 4.9 %pack.1 = (bf16[8,1056,128]{2,1,0:T(8,128)(2,1)}, s32[64]{0:T(128)}) custom-call(s32[112]{0:T(128)} %owner.3, bf16[112,64,128]{2,1,0:T(8,128)(2,1)} %bitcast.75, bf16[8,32,128]{2,1,0:T(8,128)(2,1)} %bitcast.81), custom_call_target="tpu_custom_call" | custom-call | tf_op jit(solution)/shard_map/pack/pallas_call | solution.py:237
  5.6 38.1 %all_to_all.25.got = bf16[8,1056,128]{2,1,0:T(8,128)(2,1)} all-to-all(bf16[8,1056,128]{2,1,0:T(8,128)(2,1)} %get-tuple-element.21), channel_id=1, replica_groups={{0,8,16,24,32,40,48,56},{2,10,18,26,34,42,50,58},{4,12,20,28,36,44,52,6..., dimensions={0} | all-to-all | bytes 4325376 | tf_op jit(solution)/shard_map/all_to_all | solution.py:216
  43.6 2.7 %partial_sum.1 = f32[8,136,128]{2,1,0:T(8,128)} custom-call(bf16[8,1056,128]{2,1,0:T(8,128)(2,1)} %all_to_all.25.got), custom_call_target="tpu_custom_call" | custom-call | tf_op jit(solution)/shard_map/partial_sum/pallas_call | solution.py:246
  46.3 24.1 %all_to_all.26.got = f32[8,136,128]{2,1,0:T(8,128)} all-to-all(f32[8,136,128]{2,1,0:T(8,128)} %partial_sum.1), channel_id=1, replica_groups={{0,64,128,192,256,320,384,448},{2,66,130,194,258,322,386,450},{4,68,132..., dimensions={0} | all-to-all | bytes 1114112 | tf_op jit(solution)/shard_map/all_to_all | solution.py:216
  70.4 1.9 %update.1 = (f32[128,128]{1,0:T(8,128)}, f32[128,128]{1,0:T(8,128)}, f32[128,128]{1,0:T(8,128)}, f32[8,8,128]{2,1,0:T(8,128)}, f32[8,128]{1,0:T(8,128)}) custom-call(s32[64]{0:T(128)} %get-tuple-element.20.held, f32[8,136,128]{2,1,0:T(8,128)} %all_to_all.26.got, f32[128,128]{1,0:T(8,128)} %bitcast.76, f32[128,128]{1,0:T(8,128)} %bitcast.82, f32[128,128]{1,0:T(8,128)} %bitcast.83), custom_call_target="tpu_custom_call" | custom-call | tf_op jit(solution)/shard_map/update/pallas_call | solution.py:256
  72.2 8.9 %all_to_all.27.norms = f32[8,8,128]{2,1,0:T(8,128)} all-to-all(f32[8,8,128]{2,1,0:T(8,128)} %get-tuple-element.22), channel_id=1, replica_groups=mesh['dp'=64,'own'=8] {'own'}, dimensions={0} | all-to-all | bytes 65536 | tf_op jit(solution)/shard_map/all_to_all | solution.py:275
  81.2 1.8 %step.1 = (f32[128,128]{1,0:T(8,128)}, bf16[8,136,128]{2,1,0:T(8,128)(2,1)}) custom-call(s32[64]{0:T(128)} %get-tuple-element.20.held, f32[8,8,128]{2,1,0:T(8,128)} %all_to_all.27.norms, f32[128,128]{1,0:T(8,128)} %bitcast.77, f32[128,128]{1,0:T(8,128)} %get-tuple-element.23.update, f32[8,128]{1,0:T(8,128)} %get-tuple-element.24.vec), custom_call_target="tpu_custom_call" | custom-call | tf_op jit(solution)/shard_map/step/pallas_call | solution.py:276
  83.0 14.7 %all_to_all.28.got = bf16[8,136,128]{2,1,0:T(8,128)(2,1)} all-to-all(bf16[8,136,128]{2,1,0:T(8,128)(2,1)} %get-tuple-element.28), channel_id=1, replica_groups={{0,64,128,192,256,320,384,448},{2,66,130,194,258,322,386,450},{4,68,132..., dimensions={0} | all-to-all | bytes 557056 | tf_op jit(solution)/shard_map/all_to_all | solution.py:216
  97.6 2.6 %repeat.1 = bf16[8,1088,128]{2,1,0:T(8,128)(2,1)} custom-call(bf16[8,136,128]{2,1,0:T(8,128)(2,1)} %all_to_all.28.got), custom_call_target="tpu_custom_call" | custom-call | tf_op jit(solution)/shard_map/repeat/pallas_call | solution.py:284
  100.2 35.9 %all_to_all.29.got = bf16[8,1088,128]{2,1,0:T(8,128)(2,1)} all-to-all(bf16[8,1088,128]{2,1,0:T(8,128)(2,1)} %repeat.1), channel_id=1, replica_groups={{0,8,16,24,32,40,48,56},{2,10,18,26,34,42,50,58},{4,12,20,28,36,44,52,6..., dimensions={0} | all-to-all | bytes 4456448 | tf_op jit(solution)/shard_map/all_to_all | solution.py:216
  136.1 4.5 %unpack.1 = (bf16[112,64,128]{2,1,0:T(8,128)(2,1)}, f32[8,32,128]{2,1,0:T(8,128)}, f32[8,32,128]{2,1,0:T(8,128)}, f32[8,32,128]{2,1,0:T(8,128)}) custom-call(s32[112]{0:T(128)} %owner.3, bf16[8,1088,128]{2,1,0:T(8,128)(2,1)} %all_to_all.29.got, f32[8,32,128]{2,1,0:T(8,128)} %bitcast.78, f32[8,32,128]{2,1,0:T(8,128)} %bitcast.79, f32[8,32,128]{2,1,0:T(8,128)} %bitcast.80), custom_call_target="tpu_custom_call" | custom-call | tf_op jit(solution)/shard_map/unpack/pallas_call | solution.py:293

commit v2 on v1

--- a/solution.py
+++ b/solution.py
@@ -30,48 +30,61 @@
 ANY = pl.BlockSpec(memory_space=pl.ANY)
 
 
-def place_of(group):
+def strides(far, near):
     core = lax.rem(lax.axis_index("own"), 2)
-    z, y = group // SIDE, lax.rem(group, SIDE)
-    return jnp.where(core == 0, y, z), jnp.where(core == 0, z, y)
-
-
-def pack_kernel(owner, grads, vecs, out, held, sem, vec_sem):
+    return jnp.where(core == 0, near, far), jnp.where(core == 0, far, near)
+
+
+def row_of(slot, by_z, by_y, tile):
+    z = lax.shift_right_logical(slot, 4)
+    y = lax.shift_right_logical(slot, 1) & (SIDE - 1)
+    return pl.multiple_of(z * by_z + y * by_y + (slot & 1) * ROWS, tile)
+
+
+def pack_kernel(owner, grads, vecs, out, slots, held, blank, sem):
     count = owner.shape[0]
+    by_z, by_y = strides(WIDE, SLOT_ROWS)
+    for far in range(SIDE):
+        pltpu.make_async_copy(vecs.at[far], out.at[pl.ds(far * WIDE + PART, SIDE * VEC_ROWS), :], sem).start()
+    blank[...] = jnp.zeros_like(blank)
 
     def clear(g, _):
         held[g] = 0
         return 0
 
-    lax.fori_loop(0, SIDE * SIDE, clear, 0, unroll=8)
-    vec_copy = pltpu.make_async_copy(vecs, out.at[:, pl.ds(PART, SIDE * VEC_ROWS), :], vec_sem)
-    vec_copy.start()
+    lax.fori_loop(0, SIDE * SIDE, clear, 0, unroll=16)
 
     def send(m, _):
         g = owner[m]
         rank = held[g]
         held[g] = rank + 1
-        far, near = place_of(g)
-        row = pl.multiple_of(near * SLOT_ROWS + rank * ROWS, ROWS)
-        pltpu.make_async_copy(grads.at[m], out.at[far, pl.ds(row, ROWS), :], sem).start()
+        slot = g * CAP + rank
+        slots[m] = slot
+        row = row_of(slot, by_z, by_y, 32)
+        pltpu.make_async_copy(grads.at[m], out.at[pl.ds(row, ROWS), :], sem).start()
         return 0
 
-    lax.fori_loop(0, count, send, 0, unroll=4)
+    lax.fori_loop(0, count, send, 0, unroll=8)
 
     def empty(g, _):
-        far, near = place_of(g)
-        for rank in range(CAP):
-
-            @pl.when(held[g] <= rank)
+        filled = held[g]
+
+        @pl.when(filled < CAP)
+        def _():
+            def put(slot):
+                row = row_of(slot, by_z, by_y, 32)
+                pltpu.make_async_copy(blank, out.at[pl.ds(row, ROWS), :], sem).start()
+
+            put(g * CAP + 1)
+
+            @pl.when(filled == 0)
             def _():
-                row = pl.multiple_of(near * SLOT_ROWS + rank * ROWS, ROWS)
-                out[far, pl.ds(row, ROWS), :] = jnp.zeros((ROWS, LANES), out.dtype)
+                put(g * CAP)
 
         return 0
 
-    lax.fori_loop(0, SIDE * SIDE, empty, 0, unroll=2)
-    vec_copy.wait()
-    pltpu.make_async_copy(grads, grads, sem).wait()
+    lax.fori_loop(0, SIDE * SIDE, empty, 0, unroll=4)
+    pltpu.make_async_copy(out, out, sem).wait()
 
 
 def partial_sum_kernel(got, out):
@@ -146,31 +159,22 @@
             out[k, pl.ds(near * CHUNK, CHUNK), :] = block
 
 
-def unpack_kernel(owner, got, vec_master, vec_first, vec_second, weights, new_master, new_first, new_second, held, sem):
-    count = owner.shape[0]
-
-    def clear(g, _):
-        held[g] = 0
+def unpack_kernel(slots, got, vec_master, vec_first, vec_second, weights, new_master, new_first, new_second, parts, sem, part_sem):
+    count = slots.shape[0]
+    by_z, by_y = strides(SIDE * CHUNK, CHUNK)
+    for k in range(SIDE * SIDE):
+        pltpu.make_async_copy(got.at[pl.ds(k * CHUNK + SLOT_ROWS, 2 * VEC_ROWS), :], parts.at[k], part_sem).start()
+
+    def fetch(m, _):
+        row = row_of(slots[m], by_z, by_y, 8)
+        pltpu.make_async_copy(got.at[pl.ds(row, ROWS), :], weights.at[m], sem).start()
         return 0
 
-    lax.fori_loop(0, SIDE * SIDE, clear, 0, unroll=8)
-
-    def fetch(m, _):
-        g = owner[m]
-        rank = held[g]
-        held[g] = rank + 1
-        far, near = place_of(g)
-        row = pl.multiple_of(near * CHUNK + rank * ROWS, 8)
-        pltpu.make_async_copy(got.at[far, pl.ds(row, ROWS), :], weights.at[m], sem).start()
-        return 0
-
-    lax.fori_loop(0, count, fetch, 0, unroll=4)
+    lax.fori_loop(0, count, fetch, 0, unroll=8)
+    pltpu.make_async_copy(parts, parts, part_sem).wait()
     for far in range(SIDE):
-        pieces = []
-        for near in range(SIDE):
-            both = got[far, pl.ds(near * CHUNK + SLOT_ROWS, 2 * VEC_ROWS), :].astype(jnp.float32)
-            pieces.append(both[:VEC_ROWS] + both[VEC_ROWS:])
-        gradient = jnp.concatenate(pieces, axis=0)
+        both = parts[pl.ds(far * SIDE, SIDE)].astype(jnp.float32)
+        gradient = (both[:, :VEC_ROWS] + both[:, VEC_ROWS:]).reshape(SIDE * VEC_ROWS, LANES)
         first = beta_one * vec_first[far] + (1.0 - beta_one) * gradient
         second = beta_two * vec_second[far] + (1.0 - beta_two) * gradient * gradient
         new_first[far] = first
@@ -218,6 +222,10 @@
 
 def vmem(shape, dtype):
     return pltpu.VMEM(shape, dtype)
+
+
+def close(x):
+    return pltpu.with_memory_space_constraint(x, pltpu.VMEM)
 
 
 def body(
@@ -234,33 +242,37 @@
     f32, bf16 = jnp.float32, jnp.bfloat16
     first_groups, second_groups = axis_groups()
     count = owner_group.shape[0]
-    packed, held = pl.pallas_call(
+    packed, slots, held = pl.pallas_call(
         pack_kernel,
-        out_shape=(jax.ShapeDtypeStruct((SIDE, WIDE, LANES), bf16), jax.ShapeDtypeStruct((SIDE * SIDE,), jnp.int32)),
+        out_shape=(
+            jax.ShapeDtypeStruct((SIDE * WIDE, LANES), bf16),
+            jax.ShapeDtypeStruct((count,), jnp.int32),
+            jax.ShapeDtypeStruct((SIDE * SIDE,), jnp.int32),
+        ),
         in_specs=[SMEM, ANY, ANY],
-        out_specs=(VMEM, SMEM),
-        scratch_shapes=[pltpu.SemaphoreType.DMA, pltpu.SemaphoreType.DMA],
+        out_specs=(ANY, SMEM, SMEM),
+        scratch_shapes=[pltpu.VMEM((ROWS, LANES), bf16), pltpu.SemaphoreType.DMA],
         name="pack",
     )(owner_group, to_rows(partial_grads[0]), vec_rows(vec_grads[0]))
-    got = exchange(packed, first_groups)
+    got = close(exchange(packed.reshape(SIDE, WIDE, LANES), first_groups))
     partial = pl.pallas_call(
         partial_sum_kernel,
-        out_shape=jax.ShapeDtypeStruct((SIDE, CHUNK, LANES), f32),
+        out_shape=vmem((SIDE, CHUNK, LANES), f32),
         in_specs=[VMEM],
         out_specs=VMEM,
         name="partial_sum",
     )(got)
-    got = exchange(partial, second_groups)
+    got = close(exchange(partial, second_groups))
     block = jax.ShapeDtypeStruct((SLOT_ROWS, LANES), f32)
-    master_rows = to_rows(master).reshape(SLOT_ROWS, LANES)
+    master_rows = close(to_rows(master).reshape(SLOT_ROWS, LANES))
     new_first, new_second, update, norms, vec_sum = pl.pallas_call(
         update_kernel,
         out_shape=(
             block,
             block,
-            block,
-            jax.ShapeDtypeStruct((SIDE, 8, LANES), f32),
-            jax.ShapeDtypeStruct((2 * VEC_ROWS, LANES), f32),
+            vmem((SLOT_ROWS, LANES), f32),
+            vmem((SIDE, 8, LANES), f32),
+            vmem((2 * VEC_ROWS, LANES), f32),
         ),
         in_specs=[SMEM] + [VMEM] * 4,
         out_specs=(VMEM,) * 5,
@@ -269,43 +281,47 @@
         held,
         got,
         master_rows,
-        to_rows(moment_one).reshape(SLOT_ROWS, LANES),
-        to_rows(moment_two).reshape(SLOT_ROWS, LANES),
+        close(to_rows(moment_one).reshape(SLOT_ROWS, LANES)),
+        close(to_rows(moment_two).reshape(SLOT_ROWS, LANES)),
     )
-    norms = lax.all_to_all(norms, "own", 0, 0, tiled=True)
+    norms = close(lax.all_to_all(norms, "own", 0, 0, tiled=True))
     new_master, out = pl.pallas_call(
         step_kernel,
-        out_shape=(block, jax.ShapeDtypeStruct((SIDE, CHUNK, LANES), bf16)),
+        out_shape=(block, vmem((SIDE, CHUNK, LANES), bf16)),
         in_specs=[SMEM] + [VMEM] * 4,
         out_specs=(VMEM, VMEM),
         name="step",
     )(held, norms, master_rows, update, vec_sum)
-    got = exchange(out, second_groups)
+    got = close(exchange(out, second_groups))
     out = pl.pallas_call(
         repeat_kernel,
-        out_shape=jax.ShapeDtypeStruct((SIDE, SIDE * CHUNK, LANES), bf16),
+        out_shape=vmem((SIDE, SIDE * CHUNK, LANES), bf16),
         in_specs=[VMEM],
         out_specs=VMEM,
         name="repeat",
     )(got)
-    got = exchange(out, first_groups)
+    got = exchange(out, first_groups).reshape(SIDE * SIDE * CHUNK, LANES)
     vec_block = jax.ShapeDtypeStruct((SIDE, 4 * SIDE, LANES), f32)
     weights, new_vec_master, new_vec_first, new_vec_second = pl.pallas_call(
         unpack_kernel,
         out_shape=(jax.ShapeDtypeStruct((count, ROWS, LANES), bf16), vec_block, vec_block, vec_block),
-        in_specs=[SMEM, VMEM, VMEM, VMEM, VMEM],
+        in_specs=[SMEM, ANY, VMEM, VMEM, VMEM],
         out_specs=(ANY, VMEM, VMEM, VMEM),
-        scratch_shapes=[pltpu.SMEM((SIDE * SIDE,), jnp.int32), pltpu.SemaphoreType.DMA],
+        scratch_shapes=[
+            pltpu.VMEM((SIDE * SIDE, 2 * VEC_ROWS, LANES), bf16),
+            pltpu.SemaphoreType.DMA,
+            pltpu.SemaphoreType.DMA,
+        ],
         name="unpack",
-    )(owner_group, got, vec_rows(vec_master), vec_rows(vec_first), vec_rows(vec_second))
-
-    def slots(rows):
+    )(slots, got, *(close(vec_rows(x)) for x in (vec_master, vec_first, vec_second)))
+
+    def blocks(rows):
         return from_rows(rows.reshape(CAP, ROWS, LANES))
 
     return (
-        slots(new_master),
-        slots(new_first),
-        slots(new_second),
+        blocks(new_master),
+        blocks(new_first),
+        blocks(new_second),
         from_rows(weights),
         from_vec_rows(new_vec_master),
         from_vec_rows(new_vec_first),

time: 141 us -> 241 us (1.71)
  Pallas kernels: 18.4 us -> 122 us
  blocking collectives: 122 us -> 118 us
    pallas_call x1, Pallas kernels: 4.48 us -> 58.2 us  [body(): pl.pallas_call(unpack_kernel, out_shape=(jax.ShapeDtypeStruct((count, ROW...]
    pallas_call x5, Pallas kernels: 13.9 us -> 63.4 us  [the longest x1 59.9 us: body(): pl.pallas_call(pack_kernel, out_shape=(jax.ShapeDtypeStruct((SIDE * WIDE,...]
    all_to_all x4, blocking collectives: 113 us -> 110 us  [exchange(): lax.all_to_all(x, ('dp', 'own'), 0, 0, axis_index_groups=groups, tiled=True)]
where the time goes in v2:
time: 241 us
  Pallas kernels  122 us (51%)
  blocking collectives  118 us (49%)
    all_to_all x4, blocking collectives, exchange(): lax.all_to_all(x, ('dp', 'own'), 0, 0, axis_index_groups=groups, tiled=True)  110 us
    pallas_call x1, Pallas kernels, body(): pl.pallas_call(pack_kernel, out_shape=(jax.ShapeDtypeStruct((SIDE * WIDE,...  59.9 us
    pallas_call x1, Pallas kernels, body(): pl.pallas_call(unpack_kernel, out_shape=(jax.ShapeDtypeStruct((count, ROW...  58.2 us
    all_to_all x1, blocking collectives, body(): norms = close(lax.all_to_all(norms, 'own', 0, 0, tiled=True))  8.61 us

profile of v2, /device:TPU:2, one launch (start us, length us, event | category | flops | bytes accessed | tf_op | source)
XLA Modules:
  0.0 240.6 jit_solution(4914788620308669164)
XLA Ops:
  0.6 59.9 %pack.1 = (bf16[8448,128]{1,0:T(8,128)(2,1)}, s32[112]{0:T(128)}, s32[64]{0:T(128)}) custom-call(s32[112]{0:T(128)} %owner.1, bf16[112,64,128]{2,1,0:T(8,128)(2,1)} %bitcast.86, bf16[8,32,128]{2,1,0:T(8,128)(2,1)} %bitcast.87), custom_call_target="tpu_custom_call" | custom-call | tf_op jit(solution)/shard_map/pack/pallas_call | solution.py:245
  60.5 38.0 %all_to_all.25.got = bf16[8,1056,128]{2,1,0:T(8,128)(2,1)S(1)} all-to-all(bf16[8,1056,128]{2,1,0:T(8,128)(2,1)} %bitcast.85), channel_id=1, replica_groups={{0,8,16,24,32,40,48,56},{2,10,18,26,34,42,50,58},{4,12,20,28,36,44,52,6..., dimensions={0} | all-to-all | bytes 4325376 | tf_op jit(solution)/shard_map/all_to_all | solution.py:220
  98.5 0.0 copy-start
  98.5 0.0 copy-start.4
  98.5 0.0 copy-start.5
  98.5 0.3 partial_sum.1
  98.7 23.8 %all_to_all.26.got = f32[8,136,128]{2,1,0:T(8,128)S(1)} all-to-all(f32[8,136,128]{2,1,0:T(8,128)S(1)} %partial_sum.1), channel_id=1, replica_groups={{0,64,128,192,256,320,384,448},{2,66,130,194,258,322,386,450},{4,68,132..., dimensions={0} | all-to-all | bytes 1114112 | tf_op jit(solution)/shard_map/all_to_all | solution.py:220
  122.5 0.0 copy-done
  122.5 0.0 copy-done.4
  122.5 0.0 copy-done.5
  122.5 1.4 update.1
  123.9 0.0 copy-start.6
  123.9 0.0 copy-start.7
  123.9 8.6 %all_to_all.27.norms = f32[8,8,128]{2,1,0:T(8,128)S(1)} all-to-all(f32[8,8,128]{2,1,0:T(8,128)S(1)} %get-tuple-element.23), channel_id=1, replica_groups=mesh['dp'=64,'own'=8] {'own'}, dimensions={0} | all-to-all | bytes 65536 | tf_op jit(solution)/shard_map/all_to_all | solution.py:287
  132.5 0.0 copy-done.6
  132.5 0.0 copy-done.7
  132.5 1.6 step.1
  134.1 13.0 %all_to_all.28.got = bf16[8,136,128]{2,1,0:T(8,128)(2,1)S(1)} all-to-all(bf16[8,136,128]{2,1,0:T(8,128)(2,1)S(1)} %get-tuple-element.30), channel_id=1, replica_groups={{0,64,128,192,256,320,384,448},{2,66,130,194,258,322,386,450},{4,68,132..., dimensions={0} | all-to-all | bytes 557056 | tf_op jit(solution)/shard_map/all_to_all | solution.py:220
  147.2 0.3 repeat.1
  147.5 0.0 copy-start.1
  147.5 0.0 copy-start.2
  147.5 0.0 copy-start.3
  147.5 34.8 %all_to_all.29 = bf16[8,1088,128]{2,1,0:T(8,128)(2,1)} all-to-all(bf16[8,1088,128]{2,1,0:T(8,128)(2,1)S(1)} %repeat.1), channel_id=1, replica_groups={{0,8,16,24,32,40,48,56},{2,10,18,26,34,42,50,58},{4,12,20,28,36,44,52,6..., dimensions={0} | all-to-all | bytes 4456448 | tf_op jit(solution)/shard_map/all_to_all | solution.py:220
  182.3 0.0 copy-done.1
  182.3 0.0 copy-done.2
  182.3 0.0 copy-done.3
  182.3 58.2 %unpack.1 = (bf16[112,64,128]{2,1,0:T(8,128)(2,1)}, f32[8,32,128]{2,1,0:T(8,128)}, f32[8,32,128]{2,1,0:T(8,128)}, f32[8,32,128]{2,1,0:T(8,128)}) custom-call(s32[112]{0:T(128)} %get-tuple-element.29.slots, bf16[8704,128]{1,0:T(8,128)(2,1)} %bitcast.84, f32[8,32,128]{2,1,0:T(8,128)S(1)} %bitcast.79, f32[8,32,128]{2,1,0:T(8,128)S(1)} %bitcast.80, ...), custom_call_target="tpu_custom_call" | custom-call | tf_op jit(solution)/shard_map/unpack/pallas_call | solution.py:305
Async XLA Ops:
  98.5 24.0 %copy-start = (f32[2,2,4096]{2,1,0:T(2,128)S(1)}, f32[2,2,4096]{2,1,0:T(2,128)}, u32[]{:S(2)}) copy-start(f32[2,2,4096]{2,1,0:T(2,128)} %param.11) | copy-start | bytes 196612
  98.5 24.0 %copy-start.4 = (f32[2,2,4096]{2,1,0:T(2,128)S(1)}, f32[2,2,4096]{2,1,0:T(2,128)}, u32[]{:S(2)}) copy-start(f32[2,2,4096]{2,1,0:T(2,128)} %param.12) | copy-start | bytes 196612
  98.5 24.0 %copy-start.5 = (f32[2,2,4096]{2,1,0:T(2,128)S(1)}, f32[2,2,4096]{2,1,0:T(2,128)}, u32[]{:S(2)}) copy-start(f32[2,2,4096]{2,1,0:T(2,128)} %param.13) | copy-start | bytes 196612
  123.9 8.6 %copy-start.6 = (f32[128,128]{1,0:T(8,128)}, f32[128,128]{1,0:T(8,128)S(1)}, u32[]{:S(2)}) copy-start(f32[128,128]{1,0:T(8,128)S(1)} %get-tuple-element.24.update) | copy-start | bytes 196612
  123.9 8.6 %copy-start.7 = (f32[8,128]{1,0:T(8,128)}, f32[8,128]{1,0:T(8,128)S(1)}, u32[]{:S(2)}) copy-start(f32[8,128]{1,0:T(8,128)S(1)} %get-tuple-element.25.vec) | copy-start | bytes 12292
  147.5 34.9 %copy-start.1 = (f32[64,512]{1,0:T(8,128)S(1)}, f32[64,512]{1,0:T(8,128)}, u32[]{:S(2)}) copy-start(f32[64,512]{1,0:T(8,128)} %param.15) | copy-start | bytes 393220
  147.5 34.9 %copy-start.2 = (f32[64,512]{1,0:T(8,128)S(1)}, f32[64,512]{1,0:T(8,128)}, u32[]{:S(2)}) copy-start(f32[64,512]{1,0:T(8,128)} %param.16) | copy-start | bytes 393220
  147.5 34.9 %copy-start.3 = (f32[64,512]{1,0:T(8,128)S(1)}, f32[64,512]{1,0:T(8,128)}, u32[]{:S(2)}) copy-start(f32[64,512]{1,0:T(8,128)} %param.17) | copy-start | bytes 393220

commit v3 on v2

--- a/solution.py
+++ b/solution.py
@@ -24,6 +24,7 @@
 PART = SIDE * SLOT_ROWS
 WIDE = PART + SIDE * VEC_ROWS
 CHUNK = SLOT_ROWS + 2 * VEC_ROWS
+BATCHES = 4
 
 VMEM = pl.BlockSpec(memory_space=pltpu.VMEM)
 SMEM = pl.BlockSpec(memory_space=pltpu.SMEM)
@@ -41,12 +42,11 @@
     return pl.multiple_of(z * by_z + y * by_y + (slot & 1) * ROWS, tile)
 
 
-def pack_kernel(owner, grads, vecs, out, slots, held, blank, sem):
+def pack_kernel(owner, grads, vecs, out, slots, held, sem):
     count = owner.shape[0]
     by_z, by_y = strides(WIDE, SLOT_ROWS)
     for far in range(SIDE):
         pltpu.make_async_copy(vecs.at[far], out.at[pl.ds(far * WIDE + PART, SIDE * VEC_ROWS), :], sem).start()
-    blank[...] = jnp.zeros_like(blank)
 
     def clear(g, _):
         held[g] = 0
@@ -73,7 +73,7 @@
         def _():
             def put(slot):
                 row = row_of(slot, by_z, by_y, 32)
-                pltpu.make_async_copy(blank, out.at[pl.ds(row, ROWS), :], sem).start()
+                out[pl.ds(row, ROWS), :] = jnp.zeros((ROWS, LANES), out.dtype)
 
             put(g * CAP + 1)
 
@@ -84,16 +84,25 @@
         return 0
 
     lax.fori_loop(0, SIDE * SIDE, empty, 0, unroll=4)
-    pltpu.make_async_copy(out, out, sem).wait()
-
-
-def partial_sum_kernel(got, out):
+    filled_rows = out.at[pl.ds(0, count * ROWS + SIDE * SIDE * VEC_ROWS), :]
+    pltpu.make_async_copy(filled_rows, filled_rows, sem).wait()
+
+
+def partial_sum_kernel(source, out, got, sems):
+    def piece(k):
+        rows = pl.ds(k * SLOT_ROWS, SLOT_ROWS if k < SIDE else SIDE * VEC_ROWS)
+        return pltpu.make_async_copy(source.at[:, rows, :], got.at[:, rows, :], sems.at[k])
+
+    for k in range(SIDE + 1):
+        piece(k).start()
     for near in range(SIDE):
+        piece(near).wait()
         rows = pl.ds(near * SLOT_ROWS, SLOT_ROWS)
         total = got[0, rows, :].astype(jnp.float32)
         for far in range(1, SIDE):
             total = total + got[far, rows, :].astype(jnp.float32)
         out[near, pl.ds(0, SLOT_ROWS), :] = total
+    piece(SIDE).wait()
     total = got[0, pl.ds(PART, SIDE * VEC_ROWS), :].astype(jnp.float32)
     for far in range(1, SIDE):
         total = total + got[far, pl.ds(PART, SIDE * VEC_ROWS), :].astype(jnp.float32)
@@ -159,28 +168,49 @@
             out[k, pl.ds(near * CHUNK, CHUNK), :] = block
 
 
-def unpack_kernel(slots, got, vec_master, vec_first, vec_second, weights, new_master, new_first, new_second, parts, sem, part_sem):
+def unpack_kernel(slots, got, vec_master, vec_first, vec_second, weights, new_master, new_first, new_second, staged, parts, results, in_sems, out_sems, part_sem, result_sems):
     count = slots.shape[0]
-    by_z, by_y = strides(SIDE * CHUNK, CHUNK)
-    for k in range(SIDE * SIDE):
-        pltpu.make_async_copy(got.at[pl.ds(k * CHUNK + SLOT_ROWS, 2 * VEC_ROWS), :], parts.at[k], part_sem).start()
-
-    def fetch(m, _):
-        row = row_of(slots[m], by_z, by_y, 8)
-        pltpu.make_async_copy(got.at[pl.ds(row, ROWS), :], weights.at[m], sem).start()
-        return 0
-
-    lax.fori_loop(0, count, fetch, 0, unroll=8)
-    pltpu.make_async_copy(parts, parts, part_sem).wait()
+    batch = count // BATCHES
+    by_z, by_y = strides(SIDE, 1)
+    vec_rows_of = pltpu.make_async_copy(got.at[:, pl.ds(SLOT_ROWS, 2 * VEC_ROWS), :], parts, part_sem)
+    vec_rows_of.start()
+
+    for q in range(BATCHES):
+
+        def fetch(m, _):
+            slot = slots[m]
+            z = lax.shift_right_logical(slot, 4)
+            y = lax.shift_right_logical(slot, 1) & (SIDE - 1)
+            row = pl.multiple_of((slot & 1) * ROWS, ROWS)
+            source = got.at[z * by_z + y * by_y, pl.ds(row, ROWS), :]
+            pltpu.make_async_copy(source, staged.at[m], in_sems.at[q]).start()
+            return 0
+
+        lax.fori_loop(q * batch, (q + 1) * batch, fetch, 0, unroll=7)
+
+    vec_rows_of.wait()
     for far in range(SIDE):
         both = parts[pl.ds(far * SIDE, SIDE)].astype(jnp.float32)
         gradient = (both[:, :VEC_ROWS] + both[:, VEC_ROWS:]).reshape(SIDE * VEC_ROWS, LANES)
         first = beta_one * vec_first[far] + (1.0 - beta_one) * gradient
         second = beta_two * vec_second[far] + (1.0 - beta_two) * gradient * gradient
-        new_first[far] = first
-        new_second[far] = second
-        new_master[far] = vec_master[far] - learn_rate * (first / fix_one) / (jnp.sqrt(second / fix_two) + epsilon)
-    pltpu.make_async_copy(weights, weights, sem).wait()
+        results[1, far] = first
+        results[2, far] = second
+        results[0, far] = vec_master[far] - learn_rate * (first / fix_one) / (jnp.sqrt(second / fix_two) + epsilon)
+    copies = [
+        pltpu.make_async_copy(results.at[k], out, result_sems.at[k])
+        for k, out in enumerate((new_master, new_first, new_second))
+    ]
+    for copy in copies:
+        copy.start()
+    for q in range(BATCHES):
+        some = pl.ds(q * batch, batch)
+        pltpu.make_async_copy(weights.at[some], staged.at[some], in_sems.at[q]).wait()
+        copy = pltpu.make_async_copy(staged.at[some], weights.at[some], out_sems.at[q])
+        copy.start()
+        copies.append(copy)
+    for copy in copies:
+        copy.wait()
 
 
 def to_rows(block):
@@ -245,21 +275,22 @@
     packed, slots, held = pl.pallas_call(
         pack_kernel,
         out_shape=(
-            jax.ShapeDtypeStruct((SIDE * WIDE, LANES), bf16),
+            vmem((SIDE * WIDE, LANES), bf16),
             jax.ShapeDtypeStruct((count,), jnp.int32),
             jax.ShapeDtypeStruct((SIDE * SIDE,), jnp.int32),
         ),
         in_specs=[SMEM, ANY, ANY],
-        out_specs=(ANY, SMEM, SMEM),
-        scratch_shapes=[pltpu.VMEM((ROWS, LANES), bf16), pltpu.SemaphoreType.DMA],
+        out_specs=(VMEM, SMEM, SMEM),
+        scratch_shapes=[pltpu.SemaphoreType.DMA],
         name="pack",
     )(owner_group, to_rows(partial_grads[0]), vec_rows(vec_grads[0]))
-    got = close(exchange(packed.reshape(SIDE, WIDE, LANES), first_groups))
+    got = exchange(packed.reshape(SIDE, WIDE, LANES), first_groups)
     partial = pl.pallas_call(
         partial_sum_kernel,
         out_shape=vmem((SIDE, CHUNK, LANES), f32),
-        in_specs=[VMEM],
+        in_specs=[ANY],
         out_specs=VMEM,
+        scratch_shapes=[pltpu.VMEM((SIDE, WIDE, LANES), bf16), pltpu.SemaphoreType.DMA((SIDE + 1,))],
         name="partial_sum",
     )(got)
     got = close(exchange(partial, second_groups))
@@ -291,7 +322,7 @@
         in_specs=[SMEM] + [VMEM] * 4,
         out_specs=(VMEM, VMEM),
         name="step",
-    )(held, norms, master_rows, update, vec_sum)
+    )(held, norms, master_rows, close(update), close(vec_sum))
     got = close(exchange(out, second_groups))
     out = pl.pallas_call(
         repeat_kernel,
@@ -300,17 +331,21 @@
         out_specs=VMEM,
         name="repeat",
     )(got)
-    got = exchange(out, first_groups).reshape(SIDE * SIDE * CHUNK, LANES)
+    got = exchange(out, first_groups).reshape(SIDE * SIDE, CHUNK, LANES)
     vec_block = jax.ShapeDtypeStruct((SIDE, 4 * SIDE, LANES), f32)
     weights, new_vec_master, new_vec_first, new_vec_second = pl.pallas_call(
         unpack_kernel,
         out_shape=(jax.ShapeDtypeStruct((count, ROWS, LANES), bf16), vec_block, vec_block, vec_block),
         in_specs=[SMEM, ANY, VMEM, VMEM, VMEM],
-        out_specs=(ANY, VMEM, VMEM, VMEM),
+        out_specs=(ANY, ANY, ANY, ANY),
         scratch_shapes=[
+            pltpu.VMEM((count, ROWS, LANES), bf16),
             pltpu.VMEM((SIDE * SIDE, 2 * VEC_ROWS, LANES), bf16),
+            pltpu.VMEM((3, SIDE, 4 * SIDE, LANES), f32),
+            pltpu.SemaphoreType.DMA((BATCHES,)),
+            pltpu.SemaphoreType.DMA((BATCHES,)),
             pltpu.SemaphoreType.DMA,
-            pltpu.SemaphoreType.DMA,
+            pltpu.SemaphoreType.DMA((3,)),
         ],
         name="unpack",
     )(slots, got, *(close(vec_rows(x)) for x in (vec_master, vec_first, vec_second)))

time: 241 us -> 130 us (0.54)
  Pallas kernels: 122 us -> 10.9 us
    pallas_call x1, Pallas kernels: 59.9 us -> 2.98 us  [body(): pl.pallas_call(pack_kernel, out_shape=(vmem((SIDE * WIDE, LANES), bf16),...]
    pallas_call x1, Pallas kernels: 58.2 us -> 3.17 us  [body(): pl.pallas_call(unpack_kernel, out_shape=(jax.ShapeDtypeStruct((count, ROW...]
where the time goes in v3:
time: 130 us
  blocking collectives  118 us (91%)
  Pallas kernels  10.9 us (8%)
    all_to_all x4, blocking collectives, exchange(): lax.all_to_all(x, ('dp', 'own'), 0, 0, axis_index_groups=groups, tiled=True)  110 us
    all_to_all x1, blocking collectives, body(): norms = close(lax.all_to_all(norms, 'own', 0, 0, tiled=True))  8.61 us
    pallas_call x1, Pallas kernels, body(): pl.pallas_call(unpack_kernel, out_shape=(jax.ShapeDtypeStruct((count, ROW...  3.17 us
    pallas_call x1, Pallas kernels, body(): pl.pallas_call(pack_kernel, out_shape=(vmem((SIDE * WIDE, LANES), bf16),...  2.98 us

profile of v3, /device:TPU:2, one launch (start us, length us, event | category | flops | bytes accessed | tf_op | source)
XLA Modules:
  0.0 129.7 jit_solution(5163551655229652892)
XLA Ops:
  0.6 3.0 %pack.1 = (bf16[8448,128]{1,0:T(8,128)(2,1)S(1)}, s32[112]{0:T(128)}, s32[64]{0:T(128)}) custom-call(s32[112]{0:T(128)} %owner.1, bf16[112,64,128]{2,1,0:T(8,128)(2,1)} %bitcast.86, bf16[8,32,128]{2,1,0:T(8,128)(2,1)} %bitcast.87), custom_call_target="tpu_custom_call" | custom-call | tf_op jit(solution)/shard_map/pack/pallas_call | solution.py:275
  3.6 37.9 %all_to_all.25.source = bf16[8,1056,128]{2,1,0:T(8,128)(2,1)} all-to-all(bf16[8,1056,128]{2,1,0:T(8,128)(2,1)S(1)} %bitcast.77), channel_id=1, replica_groups={{0,8,16,24,32,40,48,56},{2,10,18,26,34,42,50,58},{4,12,20,28,36,44,52,6..., dimensions={0} | all-to-all | bytes 4325376 | tf_op jit(solution)/shard_map/all_to_all | solution.py:250
  41.5 0.0 copy-start
  41.5 0.0 copy-start.4
  41.5 0.0 copy-start.5
  41.5 1.7 %partial_sum.1 = f32[8,136,128]{2,1,0:T(8,128)S(1)} custom-call(bf16[8,1056,128]{2,1,0:T(8,128)(2,1)} %all_to_all.25.source), custom_call_target="tpu_custom_call" | custom-call | tf_op jit(solution)/shard_map/partial_sum/pallas_call | solution.py:288
  43.2 23.8 %all_to_all.26.got = f32[8,136,128]{2,1,0:T(8,128)S(1)} all-to-all(f32[8,136,128]{2,1,0:T(8,128)S(1)} %partial_sum.1), channel_id=1, replica_groups={{0,64,128,192,256,320,384,448},{2,66,130,194,258,322,386,450},{4,68,132..., dimensions={0} | all-to-all | bytes 1114112 | tf_op jit(solution)/shard_map/all_to_all | solution.py:250
  66.9 0.0 copy-done
  66.9 0.0 copy-done.4
  66.9 0.0 copy-done.5
  66.9 1.4 %update.1 = (f32[128,128]{1,0:T(8,128)}, f32[128,128]{1,0:T(8,128)}, f32[128,128]{1,0:T(8,128)S(1)}, f32[8,8,128]{2,1,0:T(8,128)S(1)}, f32[8,128]{1,0:T(8,128)S(1)}) custom-call(s32[64]{0:T(128)} %get-tuple-element.21.held, f32[8,136,128]{2,1,0:T(8,128)S(1)} %all_to_all.26.got, f32[128,128]{1,0:T(8,128)S(1)} %bitcast.78, f32[128,128]{1,0:T(8,128)S(1)} %bitcast.83, ...), custom_call_target="tpu_custom_call" | custom-call | tf_op jit(solution)/shard_map/update/pallas_call | solution.py:299
  68.3 8.6 %all_to_all.27.norms = f32[8,8,128]{2,1,0:T(8,128)S(1)} all-to-all(f32[8,8,128]{2,1,0:T(8,128)S(1)} %get-tuple-element.23), channel_id=1, replica_groups=mesh['dp'=64,'own'=8] {'own'}, dimensions={0} | all-to-all | bytes 65536 | tf_op jit(solution)/shard_map/all_to_all | solution.py:318
  76.9 1.4 %step.1 = (f32[128,128]{1,0:T(8,128)}, bf16[8,136,128]{2,1,0:T(8,128)(2,1)S(1)}) custom-call(s32[64]{0:T(128)} %get-tuple-element.21.held, f32[8,8,128]{2,1,0:T(8,128)S(1)} %all_to_all.27.norms, f32[128,128]{1,0:T(8,128)S(1)} %bitcast.79, f32[128,128]{1,0:T(8,128)S(1)} %get-tuple-element.24.update, f32[8,128]{1,0:T(8,128)S(1)} %get-tuple-element.25.vec), custom_call_target="tpu_custom_call" | custom-call | tf_op jit(solution)/shard_map/step/pallas_call | solution.py:319
  78.3 13.0 %all_to_all.28.got = bf16[8,136,128]{2,1,0:T(8,128)(2,1)S(1)} all-to-all(bf16[8,136,128]{2,1,0:T(8,128)(2,1)S(1)} %get-tuple-element.30), channel_id=1, replica_groups={{0,64,128,192,256,320,384,448},{2,66,130,194,258,322,386,450},{4,68,132..., dimensions={0} | all-to-all | bytes 557056 | tf_op jit(solution)/shard_map/all_to_all | solution.py:250
  91.4 0.3 repeat.1
  91.7 0.0 copy-start.1
  91.7 0.0 copy-start.2
  91.7 0.0 copy-start.3
  91.7 34.9 %all_to_all.29 = bf16[8,1088,128]{2,1,0:T(8,128)(2,1)} all-to-all(bf16[8,1088,128]{2,1,0:T(8,128)(2,1)S(1)} %repeat.1), channel_id=1, replica_groups={{0,8,16,24,32,40,48,56},{2,10,18,26,34,42,50,58},{4,12,20,28,36,44,52,6..., dimensions={0} | all-to-all | bytes 4456448 | tf_op jit(solution)/shard_map/all_to_all | solution.py:250
  126.6 0.0 copy-done.1
  126.6 0.0 copy-done.2
  126.6 0.0 copy-done.3
  126.6 3.2 %unpack.1 = (bf16[112,64,128]{2,1,0:T(8,128)(2,1)}, f32[8,32,128]{2,1,0:T(8,128)}, f32[8,32,128]{2,1,0:T(8,128)}, f32[8,32,128]{2,1,0:T(8,128)}) custom-call(s32[112]{0:T(128)} %get-tuple-element.29.slots, bf16[64,136,128]{2,1,0:T(8,128)(2,1)} %bitcast.85, f32[8,32,128]{2,1,0:T(8,128)S(1)} %bitcast.80, f32[8,32,128]{2,1,0:T(8,128)S(1)} %bitcast.81, ...), custom_call_target="tpu_custom_call" | custom-call | tf_op jit(solution)/shard_map/unpack/pallas_call | solution.py:336
Async XLA Ops:
  41.5 25.4 %copy-start = (f32[2,2,4096]{2,1,0:T(2,128)S(1)}, f32[2,2,4096]{2,1,0:T(2,128)}, u32[]{:S(2)}) copy-start(f32[2,2,4096]{2,1,0:T(2,128)} %param.11) | copy-start | bytes 196612
  41.5 25.4 %copy-start.4 = (f32[2,2,4096]{2,1,0:T(2,128)S(1)}, f32[2,2,4096]{2,1,0:T(2,128)}, u32[]{:S(2)}) copy-start(f32[2,2,4096]{2,1,0:T(2,128)} %param.12) | copy-start | bytes 196612
  41.5 25.4 %copy-start.5 = (f32[2,2,4096]{2,1,0:T(2,128)S(1)}, f32[2,2,4096]{2,1,0:T(2,128)}, u32[]{:S(2)}) copy-start(f32[2,2,4096]{2,1,0:T(2,128)} %param.13) | copy-start | bytes 196612
  91.7 34.9 %copy-start.1 = (f32[64,512]{1,0:T(8,128)S(1)}, f32[64,512]{1,0:T(8,128)}, u32[]{:S(2)}) copy-start(f32[64,512]{1,0:T(8,128)} %param.15) | copy-start | bytes 393220
  91.7 34.9 %copy-start.2 = (f32[64,512]{1,0:T(8,128)S(1)}, f32[64,512]{1,0:T(8,128)}, u32[]{:S(2)}) copy-start(f32[64,512]{1,0:T(8,128)} %param.16) | copy-start | bytes 393220
  91.7 34.9 %copy-start.3 = (f32[64,512]{1,0:T(8,128)S(1)}, f32[64,512]{1,0:T(8,128)}, u32[]{:S(2)}) copy-start(f32[64,512]{1,0:T(8,128)} %param.17) | copy-start | bytes 393220

commit v4 on v3

--- a/solution.py
+++ b/solution.py
@@ -42,7 +42,7 @@
     return pl.multiple_of(z * by_z + y * by_y + (slot & 1) * ROWS, tile)
 
 
-def pack_kernel(owner, grads, vecs, out, slots, held, sem):
+def pack_kernel(owner, grads, vecs, out, slots_out, mine, slots, held, sem, slots_sem):
     count = owner.shape[0]
     by_z, by_y = strides(WIDE, SLOT_ROWS)
     for far in range(SIDE):
@@ -65,6 +65,9 @@
         return 0
 
     lax.fori_loop(0, count, send, 0, unroll=8)
+    slots_copy = pltpu.make_async_copy(slots, slots_out, slots_sem)
+    slots_copy.start()
+    mine[...] = jnp.full(mine.shape, held[lax.axis_index("dp")], jnp.int32)
 
     def empty(g, _):
         filled = held[g]
@@ -86,6 +89,7 @@
     lax.fori_loop(0, SIDE * SIDE, empty, 0, unroll=4)
     filled_rows = out.at[pl.ds(0, count * ROWS + SIDE * SIDE * VEC_ROWS), :]
     pltpu.make_async_copy(filled_rows, filled_rows, sem).wait()
+    slots_copy.wait()
 
 
 def partial_sum_kernel(source, out, got, sems):
@@ -111,8 +115,8 @@
         out[near, pl.ds(SLOT_ROWS + VEC_ROWS, VEC_ROWS), :] = jnp.zeros((VEC_ROWS, LANES), jnp.float32)
 
 
-def update_kernel(held, got, master, one, two, new_first, new_second, update_out, norms, vec_out):
-    mine = held[lax.axis_index("dp")]
+def update_kernel(mine, got, master, one, two, new_first, new_second, update_out, norms, vec_out):
+    filled = mine[pl.ds(0, 1), :]
     for slot in range(CAP):
         rows = pl.ds(slot * ROWS, ROWS)
         gradient = got[0, rows, :]
@@ -122,7 +126,7 @@
         first = beta_one * one[rows, :] + (1.0 - beta_one) * gradient
         second = beta_two * two[rows, :] + (1.0 - beta_two) * gradient * gradient
         update = first / fix_one / (jnp.sqrt(second / fix_two) + epsilon) + decay_rate * weight
-        keep = mine > slot
+        keep = filled > slot
         new_first[rows, :] = jnp.where(keep, first, 0.0)
         new_second[rows, :] = jnp.where(keep, second, 0.0)
         update_out[rows, :] = update
@@ -141,8 +145,8 @@
     vec_out[pl.ds(VEC_ROWS, VEC_ROWS), :] = total - total.astype(jnp.bfloat16).astype(jnp.float32)
 
 
-def step_kernel(held, norms, master, update, vec, new_master, out):
-    mine = held[lax.axis_index("dp")]
+def step_kernel(mine, norms, master, update, vec, new_master, out):
+    filled = mine[pl.ds(0, 1), :]
     total = norms[0]
     for k in range(1, SIDE):
         total = total + norms[k]
@@ -151,7 +155,7 @@
         rows = pl.ds(slot * ROWS, ROWS)
         ratio = jnp.sqrt(total[2 * slot : 2 * slot + 1]) / jnp.sqrt(total[2 * slot + 1 : 2 * slot + 2])
         stepped = master[rows, :] - learn_rate * ratio * update[rows, :]
-        stepped = jnp.where(mine > slot, stepped, 0.0)
+        stepped = jnp.where(filled > slot, stepped, 0.0)
         new_master[rows, :] = stepped
         rounded = stepped.astype(jnp.bfloat16)
         for k in range(SIDE):
@@ -168,12 +172,22 @@
             out[k, pl.ds(near * CHUNK, CHUNK), :] = block
 
 
-def unpack_kernel(slots, got, vec_master, vec_first, vec_second, weights, new_master, new_first, new_second, staged, parts, results, in_sems, out_sems, part_sem, result_sems):
+def unpack_kernel(
+    slots, got, vec_master, vec_first, vec_second, *rest
+):
+    blocks_in, (weights, new_master, new_first, new_second), rest = rest[:3], rest[3:7], rest[7:]
+    blocks_out, (staged, parts, results, in_sems, out_sems, part_sem, result_sems) = rest[:3], rest[3:]
     count = slots.shape[0]
     batch = count // BATCHES
     by_z, by_y = strides(SIDE, 1)
     vec_rows_of = pltpu.make_async_copy(got.at[:, pl.ds(SLOT_ROWS, 2 * VEC_ROWS), :], parts, part_sem)
     vec_rows_of.start()
+    copies = [
+        pltpu.make_async_copy(source, out, result_sems.at[3 + k])
+        for k, (source, out) in enumerate(zip(blocks_in, blocks_out))
+    ]
+    for copy in copies:
+        copy.start()
 
     for q in range(BATCHES):
 
@@ -197,12 +211,13 @@
         results[1, far] = first
         results[2, far] = second
         results[0, far] = vec_master[far] - learn_rate * (first / fix_one) / (jnp.sqrt(second / fix_two) + epsilon)
-    copies = [
+    results_out = [
         pltpu.make_async_copy(results.at[k], out, result_sems.at[k])
         for k, out in enumerate((new_master, new_first, new_second))
     ]
-    for copy in copies:
+    for copy in results_out:
         copy.start()
+    copies += results_out
     for q in range(BATCHES):
         some = pl.ds(q * batch, batch)
         pltpu.make_async_copy(weights.at[some], staged.at[some], in_sems.at[q]).wait()
@@ -272,18 +287,24 @@
     f32, bf16 = jnp.float32, jnp.bfloat16
     first_groups, second_groups = axis_groups()
     count = owner_group.shape[0]
-    packed, slots, held = pl.pallas_call(
+    packed, slots, mine = pl.pallas_call(
         pack_kernel,
         out_shape=(
             vmem((SIDE * WIDE, LANES), bf16),
             jax.ShapeDtypeStruct((count,), jnp.int32),
-            jax.ShapeDtypeStruct((SIDE * SIDE,), jnp.int32),
+            vmem((8, LANES), jnp.int32),
         ),
         in_specs=[SMEM, ANY, ANY],
-        out_specs=(VMEM, SMEM, SMEM),
-        scratch_shapes=[pltpu.SemaphoreType.DMA],
+        out_specs=(VMEM, ANY, VMEM),
+        scratch_shapes=[
+            pltpu.SMEM((count,), jnp.int32),
+            pltpu.SMEM((SIDE * SIDE,), jnp.int32),
+            pltpu.SemaphoreType.DMA,
+            pltpu.SemaphoreType.DMA,
+        ],
         name="pack",
     )(owner_group, to_rows(partial_grads[0]), vec_rows(vec_grads[0]))
+    mine = close(mine)
     got = exchange(packed.reshape(SIDE, WIDE, LANES), first_groups)
     partial = pl.pallas_call(
         partial_sum_kernel,
@@ -294,7 +315,7 @@
         name="partial_sum",
     )(got)
     got = close(exchange(partial, second_groups))
-    block = jax.ShapeDtypeStruct((SLOT_ROWS, LANES), f32)
+    block = vmem((SLOT_ROWS, LANES), f32)
     master_rows = close(to_rows(master).reshape(SLOT_ROWS, LANES))
     new_first, new_second, update, norms, vec_sum = pl.pallas_call(
         update_kernel,
@@ -305,11 +326,11 @@
             vmem((SIDE, 8, LANES), f32),
             vmem((2 * VEC_ROWS, LANES), f32),
         ),
-        in_specs=[SMEM] + [VMEM] * 4,
+        in_specs=[VMEM] * 5,
         out_specs=(VMEM,) * 5,
         name="update",
     )(
-        held,
+        mine,
         got,
         master_rows,
         close(to_rows(moment_one).reshape(SLOT_ROWS, LANES)),
@@ -319,10 +340,10 @@
     new_master, out = pl.pallas_call(
         step_kernel,
         out_shape=(block, vmem((SIDE, CHUNK, LANES), bf16)),
-        in_specs=[SMEM] + [VMEM] * 4,
+        in_specs=[VMEM] * 5,
         out_specs=(VMEM, VMEM),
         name="step",
-    )(held, norms, master_rows, close(update), close(vec_sum))
+    )(mine, norms, master_rows, close(update), close(vec_sum))
     got = close(exchange(out, second_groups))
     out = pl.pallas_call(
         repeat_kernel,
@@ -333,11 +354,12 @@
     )(got)
     got = exchange(out, first_groups).reshape(SIDE * SIDE, CHUNK, LANES)
     vec_block = jax.ShapeDtypeStruct((SIDE, 4 * SIDE, LANES), f32)
-    weights, new_vec_master, new_vec_first, new_vec_second = pl.pallas_call(
+    rows = jax.ShapeDtypeStruct((SLOT_ROWS, LANES), f32)
+    weights, new_vec_master, new_vec_first, new_vec_second, new_master, new_first, new_second = pl.pallas_call(
         unpack_kernel,
-        out_shape=(jax.ShapeDtypeStruct((count, ROWS, LANES), bf16), vec_block, vec_block, vec_block),
-        in_specs=[SMEM, ANY, VMEM, VMEM, VMEM],
-        out_specs=(ANY, ANY, ANY, ANY),
+        out_shape=(jax.ShapeDtypeStruct((count, ROWS, LANES), bf16), vec_block, vec_block, vec_block, rows, rows, rows),
+        in_specs=[SMEM, ANY] + [VMEM] * 6,
+        out_specs=(ANY,) * 7,
         scratch_shapes=[
             pltpu.VMEM((count, ROWS, LANES), bf16),
             pltpu.VMEM((SIDE * SIDE, 2 * VEC_ROWS, LANES), bf16),
@@ -345,10 +367,15 @@
             pltpu.SemaphoreType.DMA((BATCHES,)),
             pltpu.SemaphoreType.DMA((BATCHES,)),
             pltpu.SemaphoreType.DMA,
-            pltpu.SemaphoreType.DMA((3,)),
+            pltpu.SemaphoreType.DMA((6,)),
         ],
         name="unpack",
-    )(slots, got, *(close(vec_rows(x)) for x in (vec_master, vec_first, vec_second)))
+    )(
+        slots,
+        got,
+        *(close(vec_rows(x)) for x in (vec_master, vec_first, vec_second)),
+        *(close(x) for x in (new_master, new_first, new_second)),
+    )
 
     def blocks(rows):
         return from_rows(rows.reshape(CAP, ROWS, LANES))

time: 130 us -> 127 us (0.977)
  Pallas kernels: 10.9 us -> 7.96 us
where the time goes in v4:
time: 127 us
  blocking collectives  118 us (93%)
  Pallas kernels  7.96 us (6%)
    all_to_all x4, blocking collectives, exchange(): lax.all_to_all(x, ('dp', 'own'), 0, 0, axis_index_groups=groups, tiled=True)  110 us
    all_to_all x1, blocking collectives, body(): norms = close(lax.all_to_all(norms, 'own', 0, 0, tiled=True))  8.62 us
    pallas_call x1, Pallas kernels, body(): pl.pallas_call(unpack_kernel, out_shape=(jax.ShapeDtypeStruct((count, ROW...  3.27 us

profile of v4, /device:TPU:2, one launch (start us, length us, event | category | flops | bytes accessed | tf_op | source)
XLA Modules:
  0.0 126.8 jit_solution(11173773839780053621)
XLA Ops:
  0.6 2.5 %pack.1 = (bf16[8448,128]{1,0:T(8,128)(2,1)S(1)}, s32[112]{0:T(128)}, s32[8,128]{1,0:T(8,128)S(1)}) custom-call(s32[112]{0:T(128)} %owner.1, bf16[112,64,128]{2,1,0:T(8,128)(2,1)} %bitcast.86, bf16[8,32,128]{2,1,0:T(8,128)(2,1)} %bitcast.87), custom_call_target="tpu_custom_call" | custom-call | tf_op jit(solution)/shard_map/pack/pallas_call | solution.py:290
  3.1 37.9 %all_to_all.25.source = bf16[8,1056,128]{2,1,0:T(8,128)(2,1)} all-to-all(bf16[8,1056,128]{2,1,0:T(8,128)(2,1)S(1)} %bitcast.77), channel_id=1, replica_groups={{0,8,16,24,32,40,48,56},{2,10,18,26,34,42,50,58},{4,12,20,28,36,44,52,6..., dimensions={0} | all-to-all | bytes 4325376 | tf_op jit(solution)/shard_map/all_to_all | solution.py:265
  41.0 0.0 copy-start
  41.0 0.0 copy-start.4
  41.0 0.0 copy-start.5
  41.0 1.7 %partial_sum.1 = f32[8,136,128]{2,1,0:T(8,128)S(1)} custom-call(bf16[8,1056,128]{2,1,0:T(8,128)(2,1)} %all_to_all.25.source), custom_call_target="tpu_custom_call" | custom-call | tf_op jit(solution)/shard_map/partial_sum/pallas_call | solution.py:309
  42.6 23.8 %all_to_all.26.got = f32[8,136,128]{2,1,0:T(8,128)S(1)} all-to-all(f32[8,136,128]{2,1,0:T(8,128)S(1)} %partial_sum.1), channel_id=1, replica_groups={{0,64,128,192,256,320,384,448},{2,66,130,194,258,322,386,450},{4,68,132..., dimensions={0} | all-to-all | bytes 1114112 | tf_op jit(solution)/shard_map/all_to_all | solution.py:265
  66.4 0.0 copy-done
  66.4 0.0 copy-done.4
  66.4 0.0 copy-done.5
  66.4 0.1 update.1
  66.5 8.6 %all_to_all.27.norms = f32[8,8,128]{2,1,0:T(8,128)S(1)} all-to-all(f32[8,8,128]{2,1,0:T(8,128)S(1)} %get-tuple-element.27), channel_id=1, replica_groups=mesh['dp'=64,'own'=8] {'own'}, dimensions={0} | all-to-all | bytes 65536 | tf_op jit(solution)/shard_map/all_to_all | solution.py:339
  75.1 0.2 step.1
  75.3 13.1 %all_to_all.28.got = bf16[8,136,128]{2,1,0:T(8,128)(2,1)S(1)} all-to-all(bf16[8,136,128]{2,1,0:T(8,128)(2,1)S(1)} %get-tuple-element.30), channel_id=1, replica_groups={{0,64,128,192,256,320,384,448},{2,66,130,194,258,322,386,450},{4,68,132..., dimensions={0} | all-to-all | bytes 557056 | tf_op jit(solution)/shard_map/all_to_all | solution.py:265
  88.4 0.3 repeat.1
  88.7 0.0 copy-start.1
  88.7 0.0 copy-start.2
  88.7 0.0 copy-start.3
  88.7 34.9 %all_to_all.29 = bf16[8,1088,128]{2,1,0:T(8,128)(2,1)} all-to-all(bf16[8,1088,128]{2,1,0:T(8,128)(2,1)S(1)} %repeat.1), channel_id=1, replica_groups={{0,8,16,24,32,40,48,56},{2,10,18,26,34,42,50,58},{4,12,20,28,36,44,52,6..., dimensions={0} | all-to-all | bytes 4456448 | tf_op jit(solution)/shard_map/all_to_all | solution.py:265
  123.5 0.0 copy-done.1
  123.5 0.0 copy-done.2
  123.5 0.0 copy-done.3
  123.6 3.3 %unpack.1 = (bf16[112,64,128]{2,1,0:T(8,128)(2,1)}, f32[8,32,128]{2,1,0:T(8,128)}, f32[8,32,128]{2,1,0:T(8,128)}, f32[8,32,128]{2,1,0:T(8,128)}, f32[128,128]{1,...) custom-call(s32[112]{0:T(128)} %get-tuple-element.24.slots, bf16[64,136,128]{2,1,0:T(8,128)(2,1)} %bitcast.85, ...), custom_call_target="tpu_custom_call" | custom-call | tf_op jit(solution)/shard_map/unpack/pallas_call | solution.py:358
Async XLA Ops:
  41.0 25.4 %copy-start = (f32[2,2,4096]{2,1,0:T(2,128)S(1)}, f32[2,2,4096]{2,1,0:T(2,128)}, u32[]{:S(2)}) copy-start(f32[2,2,4096]{2,1,0:T(2,128)} %param.11) | copy-start | bytes 196612
  41.0 25.4 %copy-start.4 = (f32[2,2,4096]{2,1,0:T(2,128)S(1)}, f32[2,2,4096]{2,1,0:T(2,128)}, u32[]{:S(2)}) copy-start(f32[2,2,4096]{2,1,0:T(2,128)} %param.12) | copy-start | bytes 196612
  41.0 25.4 %copy-start.5 = (f32[2,2,4096]{2,1,0:T(2,128)S(1)}, f32[2,2,4096]{2,1,0:T(2,128)}, u32[]{:S(2)}) copy-start(f32[2,2,4096]{2,1,0:T(2,128)} %param.13) | copy-start | bytes 196612
  88.7 34.9 %copy-start.1 = (f32[64,512]{1,0:T(8,128)S(1)}, f32[64,512]{1,0:T(8,128)}, u32[]{:S(2)}) copy-start(f32[64,512]{1,0:T(8,128)} %param.15) | copy-start | bytes 393220
  88.7 34.9 %copy-start.2 = (f32[64,512]{1,0:T(8,128)S(1)}, f32[64,512]{1,0:T(8,128)}, u32[]{:S(2)}) copy-start(f32[64,512]{1,0:T(8,128)} %param.16) | copy-start | bytes 393220
  88.7 34.9 %copy-start.3 = (f32[64,512]{1,0:T(8,128)S(1)}, f32[64,512]{1,0:T(8,128)}, u32[]{:S(2)}) copy-start(f32[64,512]{1,0:T(8,128)} %param.17) | copy-start | bytes 393220

commit v5 on v4

--- a/solution.py
+++ b/solution.py
@@ -24,7 +24,6 @@
 PART = SIDE * SLOT_ROWS
 WIDE = PART + SIDE * VEC_ROWS
 CHUNK = SLOT_ROWS + 2 * VEC_ROWS
-BATCHES = 4
 
 VMEM = pl.BlockSpec(memory_space=pltpu.VMEM)
 SMEM = pl.BlockSpec(memory_space=pltpu.SMEM)
@@ -69,24 +68,6 @@
     slots_copy.start()
     mine[...] = jnp.full(mine.shape, held[lax.axis_index("dp")], jnp.int32)
 
-    def empty(g, _):
-        filled = held[g]
-
-        @pl.when(filled < CAP)
-        def _():
-            def put(slot):
-                row = row_of(slot, by_z, by_y, 32)
-                out[pl.ds(row, ROWS), :] = jnp.zeros((ROWS, LANES), out.dtype)
-
-            put(g * CAP + 1)
-
-            @pl.when(filled == 0)
-            def _():
-                put(g * CAP)
-
-        return 0
-
-    lax.fori_loop(0, SIDE * SIDE, empty, 0, unroll=4)
     filled_rows = out.at[pl.ds(0, count * ROWS + SIDE * SIDE * VEC_ROWS), :]
     pltpu.make_async_copy(filled_rows, filled_rows, sem).wait()
     slots_copy.wait()
@@ -122,11 +103,12 @@
         gradient = got[0, rows, :]
         for k in range(1, SIDE):
             gradient = gradient + got[k, rows, :]
+        keep = filled > slot
+        gradient = jnp.where(keep, gradient, 0.0)
         weight = master[rows, :]
         first = beta_one * one[rows, :] + (1.0 - beta_one) * gradient
         second = beta_two * two[rows, :] + (1.0 - beta_two) * gradient * gradient
         update = first / fix_one / (jnp.sqrt(second / fix_two) + epsilon) + decay_rate * weight
-        keep = filled > slot
         new_first[rows, :] = jnp.where(keep, first, 0.0)
         new_second[rows, :] = jnp.where(keep, second, 0.0)
         update_out[rows, :] = update
@@ -165,23 +147,17 @@
         out[k, pl.ds(SLOT_ROWS, 2 * VEC_ROWS), :] = rounded
 
 
-def repeat_kernel(got, out):
-    for near in range(SIDE):
-        block = got[near]
-        for k in range(SIDE):
-            out[k, pl.ds(near * CHUNK, CHUNK), :] = block
-
-
-def unpack_kernel(
-    slots, got, vec_master, vec_first, vec_second, *rest
-):
+def repeat_kernel(got, out, sem):
+    for k in range(SIDE):
+        pltpu.make_async_copy(got, out.at[k], sem).start()
+    pltpu.make_async_copy(out, out, sem).wait()
+
+
+def unpack_kernel(slots, got, vec_master, vec_first, vec_second, *rest):
     blocks_in, (weights, new_master, new_first, new_second), rest = rest[:3], rest[3:7], rest[7:]
-    blocks_out, (staged, parts, results, in_sems, out_sems, part_sem, result_sems) = rest[:3], rest[3:]
+    blocks_out, (results, sem, result_sems) = rest[:3], rest[3:]
     count = slots.shape[0]
-    batch = count // BATCHES
     by_z, by_y = strides(SIDE, 1)
-    vec_rows_of = pltpu.make_async_copy(got.at[:, pl.ds(SLOT_ROWS, 2 * VEC_ROWS), :], parts, part_sem)
-    vec_rows_of.start()
     copies = [
         pltpu.make_async_copy(source, out, result_sems.at[3 + k])
         for k, (source, out) in enumerate(zip(blocks_in, blocks_out))
@@ -189,41 +165,28 @@
     for copy in copies:
         copy.start()
 
-    for q in range(BATCHES):
-
-        def fetch(m, _):
-            slot = slots[m]
-            z = lax.shift_right_logical(slot, 4)
-            y = lax.shift_right_logical(slot, 1) & (SIDE - 1)
-            row = pl.multiple_of((slot & 1) * ROWS, ROWS)
-            source = got.at[z * by_z + y * by_y, pl.ds(row, ROWS), :]
-            pltpu.make_async_copy(source, staged.at[m], in_sems.at[q]).start()
-            return 0
-
-        lax.fori_loop(q * batch, (q + 1) * batch, fetch, 0, unroll=7)
-
-    vec_rows_of.wait()
+    def put(m, _):
+        slot = slots[m]
+        z = lax.shift_right_logical(slot, 4)
+        y = lax.shift_right_logical(slot, 1) & (SIDE - 1)
+        row = pl.multiple_of((slot & 1) * ROWS, ROWS)
+        source = got.at[z * by_z + y * by_y, pl.ds(row, ROWS), :]
+        pltpu.make_async_copy(source, weights.at[m], sem).start()
+        return 0
+
+    lax.fori_loop(0, count, put, 0, unroll=8)
     for far in range(SIDE):
-        both = parts[pl.ds(far * SIDE, SIDE)].astype(jnp.float32)
+        both = got[pl.ds(far * SIDE, SIDE), pl.ds(SLOT_ROWS, 2 * VEC_ROWS), :].astype(jnp.float32)
         gradient = (both[:, :VEC_ROWS] + both[:, VEC_ROWS:]).reshape(SIDE * VEC_ROWS, LANES)
         first = beta_one * vec_first[far] + (1.0 - beta_one) * gradient
         second = beta_two * vec_second[far] + (1.0 - beta_two) * gradient * gradient
         results[1, far] = first
         results[2, far] = second
         results[0, far] = vec_master[far] - learn_rate * (first / fix_one) / (jnp.sqrt(second / fix_two) + epsilon)
-    results_out = [
-        pltpu.make_async_copy(results.at[k], out, result_sems.at[k])
-        for k, out in enumerate((new_master, new_first, new_second))
-    ]
-    for copy in results_out:
-        copy.start()
-    copies += results_out
-    for q in range(BATCHES):
-        some = pl.ds(q * batch, batch)
-        pltpu.make_async_copy(weights.at[some], staged.at[some], in_sems.at[q]).wait()
-        copy = pltpu.make_async_copy(staged.at[some], weights.at[some], out_sems.at[q])
-        copy.start()
-        copies.append(copy)
+    for k, out in enumerate((new_master, new_first, new_second)):
+        copies.append(pltpu.make_async_copy(results.at[k], out, result_sems.at[k]))
+        copies[-1].start()
+    pltpu.make_async_copy(weights, weights, sem).wait()
     for copy in copies:
         copy.wait()
 
@@ -344,28 +307,25 @@
         out_specs=(VMEM, VMEM),
         name="step",
     )(mine, norms, master_rows, close(update), close(vec_sum))
-    got = close(exchange(out, second_groups))
+    got = close(exchange(out, second_groups).reshape(SIDE * CHUNK, LANES))
     out = pl.pallas_call(
         repeat_kernel,
-        out_shape=vmem((SIDE, SIDE * CHUNK, LANES), bf16),
+        out_shape=jax.ShapeDtypeStruct((SIDE, SIDE * CHUNK, LANES), bf16),
         in_specs=[VMEM],
-        out_specs=VMEM,
+        out_specs=ANY,
+        scratch_shapes=[pltpu.SemaphoreType.DMA],
         name="repeat",
     )(got)
-    got = exchange(out, first_groups).reshape(SIDE * SIDE, CHUNK, LANES)
+    got = close(exchange(out, first_groups).reshape(SIDE * SIDE, CHUNK, LANES))
     vec_block = jax.ShapeDtypeStruct((SIDE, 4 * SIDE, LANES), f32)
     rows = jax.ShapeDtypeStruct((SLOT_ROWS, LANES), f32)
     weights, new_vec_master, new_vec_first, new_vec_second, new_master, new_first, new_second = pl.pallas_call(
         unpack_kernel,
         out_shape=(jax.ShapeDtypeStruct((count, ROWS, LANES), bf16), vec_block, vec_block, vec_block, rows, rows, rows),
-        in_specs=[SMEM, ANY] + [VMEM] * 6,
+        in_specs=[SMEM] + [VMEM] * 7,
         out_specs=(ANY,) * 7,
         scratch_shapes=[
-            pltpu.VMEM((count, ROWS, LANES), bf16),
-            pltpu.VMEM((SIDE * SIDE, 2 * VEC_ROWS, LANES), bf16),
             pltpu.VMEM((3, SIDE, 4 * SIDE, LANES), f32),
-            pltpu.SemaphoreType.DMA((BATCHES,)),
-            pltpu.SemaphoreType.DMA((BATCHES,)),
             pltpu.SemaphoreType.DMA,
             pltpu.SemaphoreType.DMA((6,)),
         ],

time: 127 us -> 128 us (level)
  no operation moved by 1% of the time
where the time goes in v5:
time: 128 us; the launch traced here: 127 us
  blocking collectives  118 us (92%)
  Pallas kernels  8.05 us (6%)
    all_to_all x4, blocking collectives, exchange(): lax.all_to_all(x, ('dp', 'own'), 0, 0, axis_index_groups=groups, tiled=True)  110 us
    all_to_all x1, blocking collectives, body(): norms = close(lax.all_to_all(norms, 'own', 0, 0, tiled=True))  8.62 us

profile of v5, /device:TPU:2, one launch (start us, length us, event | category | flops | bytes accessed | tf_op | source)
XLA Modules:
  0.0 127.3 jit_solution(1641915293209698776)
XLA Ops:
  0.6 2.5 %pack.1 = (bf16[8448,128]{1,0:T(8,128)(2,1)S(1)}, s32[112]{0:T(128)}, s32[8,128]{1,0:T(8,128)S(1)}) custom-call(s32[112]{0:T(128)} %owner.1, bf16[112,64,128]{2,1,0:T(8,128)(2,1)} %bitcast.88, bf16[8,32,128]{2,1,0:T(8,128)(2,1)} %bitcast.89), custom_call_target="tpu_custom_call" | custom-call | tf_op jit(solution)/shard_map/pack/pallas_call | solution.py:253
  3.1 37.9 %all_to_all.25.source = bf16[8,1056,128]{2,1,0:T(8,128)(2,1)} all-to-all(bf16[8,1056,128]{2,1,0:T(8,128)(2,1)S(1)} %bitcast.79), channel_id=1, replica_groups={{0,8,16,24,32,40,48,56},{2,10,18,26,34,42,50,58},{4,12,20,28,36,44,52,6..., dimensions={0} | all-to-all | bytes 4325376 | tf_op jit(solution)/shard_map/all_to_all | solution.py:228
  41.0 0.0 copy-start
  41.0 0.0 copy-start.4
  41.0 0.0 copy-start.5
  41.0 1.7 %partial_sum.1 = f32[8,136,128]{2,1,0:T(8,128)S(1)} custom-call(bf16[8,1056,128]{2,1,0:T(8,128)(2,1)} %all_to_all.25.source), custom_call_target="tpu_custom_call" | custom-call | tf_op jit(solution)/shard_map/partial_sum/pallas_call | solution.py:272
  42.6 23.8 %all_to_all.26.got = f32[8,136,128]{2,1,0:T(8,128)S(1)} all-to-all(f32[8,136,128]{2,1,0:T(8,128)S(1)} %partial_sum.1), channel_id=1, replica_groups={{0,64,128,192,256,320,384,448},{2,66,130,194,258,322,386,450},{4,68,132..., dimensions={0} | all-to-all | bytes 1114112 | tf_op jit(solution)/shard_map/all_to_all | solution.py:228
  66.4 0.0 copy-done
  66.4 0.0 copy-done.4
  66.4 0.0 copy-done.5
  66.4 0.1 update.1
  66.5 8.6 %all_to_all.27.norms = f32[8,8,128]{2,1,0:T(8,128)S(1)} all-to-all(f32[8,8,128]{2,1,0:T(8,128)S(1)} %get-tuple-element.27), channel_id=1, replica_groups=mesh['dp'=64,'own'=8] {'own'}, dimensions={0} | all-to-all | bytes 65536 | tf_op jit(solution)/shard_map/all_to_all | solution.py:302
  75.1 0.2 step.1
  75.3 13.1 %all_to_all.28 = bf16[8,136,128]{2,1,0:T(8,128)(2,1)S(1)} all-to-all(bf16[8,136,128]{2,1,0:T(8,128)(2,1)S(1)} %get-tuple-element.30), channel_id=1, replica_groups={{0,64,128,192,256,320,384,448},{2,66,130,194,258,322,386,450},{4,68,132..., dimensions={0} | all-to-all | bytes 557056 | tf_op jit(solution)/shard_map/all_to_all | solution.py:228
  88.4 1.4 %repeat.1 = bf16[8,1088,128]{2,1,0:T(8,128)(2,1)} custom-call(bf16[1088,128]{1,0:T(8,128)(2,1)S(1)} %bitcast.80), custom_call_target="tpu_custom_call" | custom-call | tf_op jit(solution)/shard_map/repeat/pallas_call | solution.py:311
  89.8 0.0 copy-start.1
  89.8 0.0 copy-start.2
  89.8 0.0 copy-start.3
  89.8 35.2 %all_to_all.29 = bf16[8,1088,128]{2,1,0:T(8,128)(2,1)S(1)} all-to-all(bf16[8,1088,128]{2,1,0:T(8,128)(2,1)} %repeat.1), channel_id=1, replica_groups={{0,8,16,24,32,40,48,56},{2,10,18,26,34,42,50,58},{4,12,20,28,36,44,52,6..., dimensions={0} | all-to-all | bytes 4456448 | tf_op jit(solution)/shard_map/all_to_all | solution.py:228
  125.0 0.0 copy-done.1
  125.0 0.0 copy-done.2
  125.0 0.0 copy-done.3
  125.0 2.3 %unpack.1 = (bf16[112,64,128]{2,1,0:T(8,128)(2,1)}, f32[8,32,128]{2,1,0:T(8,128)}, f32[8,32,128]{2,1,0:T(8,128)}, f32[8,32,128]{2,1,0:T(8,128)}, f32[128,128]{1,...) custom-call(s32[112]{0:T(128)} %get-tuple-element.24.slots, bf16[64,136,128]{2,1,0:T(8,128)(2,1)S(1)} %bitcast.78, ...), custom_call_target="tpu_custom_call" | custom-call | tf_op jit(solution)/shard_map/unpack/pallas_call | solution.py:322
Async XLA Ops:
  41.0 25.4 %copy-start = (f32[2,2,4096]{2,1,0:T(2,128)S(1)}, f32[2,2,4096]{2,1,0:T(2,128)}, u32[]{:S(2)}) copy-start(f32[2,2,4096]{2,1,0:T(2,128)} %param.11) | copy-start | bytes 196612
  41.0 25.4 %copy-start.4 = (f32[2,2,4096]{2,1,0:T(2,128)S(1)}, f32[2,2,4096]{2,1,0:T(2,128)}, u32[]{:S(2)}) copy-start(f32[2,2,4096]{2,1,0:T(2,128)} %param.12) | copy-start | bytes 196612
  41.0 25.4 %copy-start.5 = (f32[2,2,4096]{2,1,0:T(2,128)S(1)}, f32[2,2,4096]{2,1,0:T(2,128)}, u32[]{:S(2)}) copy-start(f32[2,2,4096]{2,1,0:T(2,128)} %param.13) | copy-start | bytes 196612
  89.8 35.2 %copy-start.1 = (f32[64,512]{1,0:T(8,128)S(1)}, f32[64,512]{1,0:T(8,128)}, u32[]{:S(2)}) copy-start(f32[64,512]{1,0:T(8,128)} %param.15) | copy-start | bytes 393220
  89.8 35.2 %copy-start.2 = (f32[64,512]{1,0:T(8,128)S(1)}, f32[64,512]{1,0:T(8,128)}, u32[]{:S(2)}) copy-start(f32[64,512]{1,0:T(8,128)} %param.16) | copy-start | bytes 393220
  89.8 35.2 %copy-start.3 = (f32[64,512]{1,0:T(8,128)S(1)}, f32[64,512]{1,0:T(8,128)}, u32[]{:S(2)}) copy-start(f32[64,512]{1,0:T(8,128)} %param.17) | copy-start | bytes 393220
